TPU v7x, 256 devices: a whole 4x4x8 slice. The times are simulated.
256 devices in a mesh: row: 16 (over x_hi, z), col: 16 (over x_lo, y, core).
Axes of the slice: x: 4 (x_hi: 2, x_lo: 2; x = x_hi * 2 + x_lo), y: 4, z: 8, core: 2. Of those that a mesh axis runs over, the one named last changes fastest.
Arguments:
- log_rate: float32 [1048576], P(('row', 'col')), may hold values from -0.5 to 1
- state: float32 [1048576], P(('row', 'col')), may hold values from 0.2 to 1
- excess: float32 [1048576], P(('row', 'col')), may hold values from -0.3 to 0.3
- normal_stress: float32 [1048576], P(('row', 'col')), may hold values from 2 to 4
- rate_param: float32 [1048576], P(('row', 'col')), may hold values from 0.5 to 1
- state_param: float32 [1048576], P(('row', 'col')), may hold values from 0.5 to 1.5
- slip_length: float32 [1048576], P(('row', 'col')), may hold values from 1 to 4
- self_stiffness: float32 [1048576], P(('row', 'col')), may hold values from 0.2 to 1
- damping: float32 [1048576], P(('row', 'col')), may hold values from 1 to 2
- blocks: bfloat16 [16, 16, 512, 4096], P('row', 'col'), may hold values from -0.1796875 to 0.1796875
- pattern: int32 [16, 16, 512, 2], P('row', 'col'), may hold values from 0 to 1023
- counts: int32 [16, 16], P('row', 'col'), may hold values from 1 to 512, as said below
Outputs:
- final_log_rate: float32 [1048576], P(('row', 'col'))
- final_state: float32 [1048576], P(('row', 'col'))
- final_stress: float32 [1048576], P(('row', 'col'))
Inputs may be any that keep to these rules, and one draw needn't show every extreme that they name: `counts`: every device holds at least one live tile; some device of the first index of row holds 512.
All inputs are finite; a program needn't handle non-finite values.
Results may differ from a plain program's by a relative error of at most 0.0014.
Values may be sent and summed in bfloat16 or wider, within the bound.
No kernel may reach another device: no remote copies, remote signals or barrier semaphores. Data moves between devices by JAX's collectives and lax.ppermute only.
A program may use at most 64 MiB of HBM per device.

v0:
```python
import math

import jax
import jax.numpy as jnp
from jax import lax
from jax.sharding import PartitionSpec as P

STEPS = 2
NEWTON = 4


time_step = 0.25


def inverse_sinh(value):
    return jnp.log(value + jnp.sqrt(1.0 + value * value))


def sweep(
    kernel_tiles,
    places,
    first_slot,
    limit_slot,
    row_rates,
    col_rates,
    owner_row,
    my_col,
    per_seg,
    row_total,
    col_total,
):
    slab_length = kernel_tiles.shape[0]
    group_size = math.gcd(128, slab_length)
    row_pieces = row_rates.reshape(-1, 64)
    col_pieces = col_rates.reshape(-1, 64)

    def turn_body(turn_index, totals):
        row_acc, col_acc = totals
        begin_slot = turn_index * group_size
        block_tiles = lax.dynamic_slice_in_dim(kernel_tiles, begin_slot, group_size, 0).reshape(
            group_size, 64, 64
        )
        block_places = lax.dynamic_slice_in_dim(places, begin_slot, group_size, 0)
        row_slot = block_places[:, 0]
        col_slot = block_places[:, 1]
        slot_ids = begin_slot + jnp.arange(group_size, dtype=jnp.int32)
        active = (slot_ids >= first_slot) & (slot_ids < limit_slot)
        diagonal = (col_slot // per_seg == owner_row) & (
            row_slot == my_col * per_seg + col_slot % per_seg
        )
        direct = jnp.einsum(
            "bij,bj->bi", block_tiles, col_pieces[col_slot], preferred_element_type=jnp.float32
        )
        mirror = jnp.einsum(
            "bij,bi->bj", block_tiles, row_pieces[row_slot], preferred_element_type=jnp.float32
        )
        direct = jnp.where(active[:, None], direct, 0.0)
        mirror = jnp.where((active & jnp.logical_not(diagonal))[:, None], mirror, 0.0)
        return (row_acc.at[row_slot].add(direct), col_acc.at[col_slot].add(mirror))

    lower = jnp.maximum(first_slot, 0) // group_size
    upper = (jnp.maximum(limit_slot, 0) + group_size - 1) // group_size
    upper = jnp.maximum(upper, lower)
    return lax.fori_loop(lower, upper, turn_body, (row_total, col_total))


def friction_solve(rate_log, stress, state, normal_stress, rate_param, damping):
    for turn_index in range(NEWTON):
        speed = jnp.exp(rate_log)
        ratio = 0.5 * jnp.exp(rate_log + state / rate_param)
        misfit = stress - damping * speed - normal_stress * rate_param * inverse_sinh(ratio)
        slope = -damping * speed - normal_stress * rate_param * ratio / jnp.sqrt(
            1.0 + ratio * ratio
        )
        rate_log = rate_log - misfit / slope
    return rate_log


def on_device(
    log_rate,
    state,
    excess,
    normal_stress,
    rate_param,
    state_param,
    slip_length,
    self_stiffness,
    damping,
    blocks,
    pattern,
    counts,
):
    patches = log_rate.shape[0]
    per_seg = patches // 64
    my_row = lax.axis_index("row")
    my_col = lax.axis_index("col")
    row_count = lax.axis_size("row")
    col_count = lax.axis_size("col")
    kernel_tiles = blocks.reshape(blocks.shape[2], blocks.shape[3])
    places = pattern.reshape(pattern.shape[2], 2)
    stored = counts[0, 0]
    rate_log = log_rate
    balance = normal_stress * rate_param * inverse_sinh(
        0.5 * jnp.exp(log_rate + state / rate_param)
    ) + damping * jnp.exp(log_rate)
    stress = balance * (1.0 + excess)
    for step_index in range(STEPS):
        speed = jnp.exp(rate_log)
        pushed = (speed - 1.0).astype(jnp.bfloat16)
        row_rates = lax.all_gather(pushed, "col", axis=0, tiled=True)
        col_rates = lax.all_gather(pushed, "row", axis=0, tiled=True)
        row_total = jnp.zeros((col_count * per_seg, 64), jnp.float32)
        col_total = jnp.zeros((row_count * per_seg, 64), jnp.float32)
        row_total, col_total = sweep(
            kernel_tiles,
            places,
            0,
            stored,
            row_rates,
            col_rates,
            my_row,
            my_col,
            per_seg,
            row_total,
            col_total,
        )
        stress_rate = lax.psum_scatter(
            row_total.reshape(-1).astype(jnp.bfloat16), "col", scatter_dimension=0, tiled=True
        ).astype(jnp.float32) + lax.psum_scatter(
            col_total.reshape(-1).astype(jnp.bfloat16), "row", scatter_dimension=0, tiled=True
        ).astype(
            jnp.float32
        )
        new_stress = stress + time_step * (stress_rate - self_stiffness * (speed - 1.0))
        state = state + time_step * (state_param / slip_length) * (
            jnp.exp(-state / state_param) - speed
        )
        stress = new_stress
        rate_log = friction_solve(rate_log, stress, state, normal_stress, rate_param, damping)
    return (rate_log, state, stress)


def solution(mesh):
    in_specs = (
        P(("row", "col")),
        P(("row", "col")),
        P(("row", "col")),
        P(("row", "col")),
        P(("row", "col")),
        P(("row", "col")),
        P(("row", "col")),
        P(("row", "col")),
        P(("row", "col")),
        P("row", "col", None, None),
        P("row", "col", None, None),
        P("row", "col"),
    )
    out_specs = (P(("row", "col")), P(("row", "col")), P(("row", "col")))
    return jax.shard_map(
        on_device, mesh=mesh, in_specs=in_specs, out_specs=out_specs, check_vma=False
    )
```

profile of v0, /device:TPU:1, one launch (start us, length us, event | category | flops | bytes accessed | tf_op | source)
XLA Modules:
  0.0 812.7 jit_solution(1112874415453995245)
XLA Ops:
  7.9 0.7 add_convert_fusion
  8.6 38.1 %all_gather.12 = bf16[65536]{0:T(1024)(128)(2,1)S(1)} all-gather(bf16[4096]{0:T(1024)(128)(2,1)S(1)} %add_convert_fusion), channel_id=1, replica_groups=mesh['row'=16,'col'=16] {'row'}, dimensions={0}, use_global_device_ids=true | all-gather | bytes 139264 | tf_op jit(solution)/shard_map/all_gather | solution.py:111
  46.7 27.0 %all_gather.13 = bf16[65536]{0:T(1024)(128)(2,1)S(1)} all-gather(bf16[4096]{0:T(1024)(128)(2,1)S(1)} %add_convert_fusion), channel_id=1, replica_groups=mesh['row'=16,'col'=16] {'col'}, dimensions={0}, use_global_device_ids=true | all-gather | bytes 139264 | tf_op jit(solution)/shard_map/all_gather | solution.py:110
  73.7 6.5 copy.16
  80.4 0.9 reshape.83
  81.2 0.8 broadcast.251.clone
  82.1 0.8 broadcast.251.clone.1
  82.9 42.3 %while.28 = (s32[]{:T(128)}, f32[1024,64]{1,0:T(8,128)}, f32[1024,64]{1,0:T(8,128)}, s32[]{:T(128)}, s32[512,2]{0,1:T(2,128)S(1)}, /*index=5*/s32[]{:T(128)}, bf...) while((s32[]{:T(128)}, f32[1024,64]{1,0:T(8,128)}, ...), condition=%wide.region_3.4_spmd, body=%wide.region_0.3_spmd.sunk | while | flops 2136966 | bytes 9749571 | solution.py:64
  82.9 1.3 constant_dynamic-slice_fusion.9
  84.2 3.5 copy.45
  89.8 1.5 scatter_custom_fusion.18
  91.4 0.7 gather_fusion.1
  92.1 1.2 fusion.80
  93.9 3.1 scatter_custom_fusion.19
  97.0 1.3 constant_dynamic-slice_fusion.9
  98.3 3.5 copy.45
  101.9 0.7 gather_fusion
  103.9 1.5 scatter_custom_fusion.18
  106.2 1.2 fusion.80
  108.0 3.1 scatter_custom_fusion.19
  111.1 1.3 constant_dynamic-slice_fusion.9
  112.4 3.5 copy.45
  118.0 1.5 scatter_custom_fusion.18
  119.6 0.7 gather_fusion.1
  120.3 1.2 fusion.80
  122.1 3.1 scatter_custom_fusion.19
  125.3 1.1 convert_element_type.46
  126.4 0.8 convert_element_type.47
  127.3 1.1 convert_element_type.43
  128.4 0.8 convert_element_type.44
  131.8 147.2 %all-reduce.11.cloned.1.call-done = bf16[65536]{0:T(1024)(128)(2,1)} async-done(((bf16[65536]{0:T(1024)(128)(2,1)}), bf16[65536]{0:T(1024)(128)(2,1)}) %all-reduce.11.cloned.1.call-update) | async-done | bytes 131088
  278.9 133.4 %all-reduce.9.cloned.1.call-done = bf16[65536]{0:T(1024)(128)(2,1)} async-done(((bf16[65536]{0:T(1024)(128)(2,1)}), bf16[65536]{0:T(1024)(128)(2,1)}) %all-reduce.9.cloned.1.call-update) | async-done | bytes 131088
  412.4 1.5 fusion.48
  413.9 34.4 %all_gather.14 = bf16[65536]{0:T(1024)(128)(2,1)S(1)} all-gather(bf16[4096]{0:T(1024)(128)(2,1)S(1)} %get-tuple-element.346), channel_id=1, replica_groups=mesh['row'=16,'col'=16] {'row'}, dimensions={0}, use_global_device_ids=true | all-gather | bytes 139264 | tf_op jit(solution)/shard_map/all_gather | solution.py:111
  448.3 24.1 %all_gather.15 = bf16[65536]{0:T(1024)(128)(2,1)S(1)} all-gather(bf16[4096]{0:T(1024)(128)(2,1)S(1)} %get-tuple-element.346), channel_id=1, replica_groups=mesh['row'=16,'col'=16] {'col'}, dimensions={0}, use_global_device_ids=true | all-gather | bytes 139264 | tf_op jit(solution)/shard_map/all_gather | solution.py:110
  472.5 0.9 reshape.85
  473.4 0.8 broadcast.251
  474.2 0.8 broadcast.251.clone.2
  475.0 42.3 %while.29 = (s32[]{:T(128)}, f32[1024,64]{1,0:T(8,128)}, f32[1024,64]{1,0:T(8,128)}, s32[]{:T(128)}, s32[512,2]{0,1:T(2,128)S(1)}, /*index=5*/s32[]{:T(128)}, bf...) while((s32[]{:T(128)}, f32[1024,64]{1,0:T(8,128)}, ...), condition=%wide.region_9.10_spmd, body=%wide.region_6.9_spmd.sunk | while | flops 2136966 | bytes 9749571 | solution.py:64
  475.0 1.3 constant_dynamic-slice_fusion.11
  476.3 3.5 copy.48
  481.9 1.5 scatter_custom_fusion.22
  483.5 0.7 gather_fusion.3
  484.2 1.2 fusion.89
  486.0 3.1 scatter_custom_fusion.23
  489.1 1.3 constant_dynamic-slice_fusion.11
  490.4 3.5 copy.48
  494.0 0.7 gather_fusion.2
  496.0 1.5 scatter_custom_fusion.22
  498.3 1.2 fusion.89
  500.1 3.1 scatter_custom_fusion.23
  503.2 1.3 constant_dynamic-slice_fusion.11
  504.5 3.5 copy.48
  510.1 1.5 scatter_custom_fusion.22
  511.7 0.7 gather_fusion.3
  512.4 1.2 fusion.89
  514.2 3.1 scatter_custom_fusion.23
  517.3 1.1 convert_element_type.53
  518.4 0.8 convert_element_type.54
  519.3 1.1 convert_element_type.50
  520.4 0.8 convert_element_type.51
  521.2 150.2 %all-reduce.15.cloned.1.call-done = bf16[65536]{0:T(1024)(128)(2,1)} async-done(((bf16[65536]{0:T(1024)(128)(2,1)}), bf16[65536]{0:T(1024)(128)(2,1)}) %all-reduce.15.cloned.1.call-update) | async-done | bytes 131088
  671.4 133.2 %all-reduce.13.cloned.1.call-done = bf16[65536]{0:T(1024)(128)(2,1)} async-done(((bf16[65536]{0:T(1024)(128)(2,1)}), bf16[65536]{0:T(1024)(128)(2,1)}) %all-reduce.13.cloned.1.call-update) | async-done | bytes 131088
  804.6 1.5 divide_subtract_fusion
  (118 shorter events, 18.1 us)
Async XLA Ops:
  7.2 271.8 %all-reduce.11.cloned.1.call-start = ((), (), s32[]{:S(2)}) async-start(), calls=%async_computation.1 | async-start | bytes 262144
  73.7 9.2 %copy-start.16 = (s32[1,1,512,2]{2,3,1,0:T(2,128)S(1)}, s32[1,1,512,2]{2,3,1,0:T(2,128)}, u32[]{:S(2)}) copy-start(s32[1,1,512,2]{2,3,1,0:T(2,128)} %param.26) | copy-start | bytes 12292
  87.7 2.1 copy-start.2
  87.7 3.6 copy-start.1
  91.3 5.7 copy-start.3
  101.8 2.1 copy-start.2
  101.8 3.6 copy-start.1
  105.4 5.7 copy-start.3
  115.9 2.1 copy-start.2
  115.9 3.6 copy-start.1
  119.5 5.7 copy-start.3
  125.2 4.1 copy-start.19
  125.2 4.7 copy-start.18
  125.2 287.1 %copy-start.6 = (f32[4096]{0:T(1024)S(1)}, f32[4096]{0:T(1024)}, u32[]{:S(2)}) copy-start(f32[4096]{0:T(1024)} %param.16) | copy-start | bytes 49156
  125.2 287.1 %copy-start.7 = (f32[4096]{0:T(1024)S(1)}, f32[4096]{0:T(1024)}, u32[]{:S(2)}) copy-start(f32[4096]{0:T(1024)} %param.24) | copy-start | bytes 49156
  125.2 287.1 %copy-start.8 = (f32[4096]{0:T(1024)S(1)}, f32[4096]{0:T(1024)}, u32[]{:S(2)}) copy-start(f32[4096]{0:T(1024)} %param.20) | copy-start | bytes 49156
  125.2 287.1 %copy-start.9 = (f32[4096]{0:T(1024)S(1)}, f32[4096]{0:T(1024)}, u32[]{:S(2)}) copy-start(f32[4096]{0:T(1024)} %param.17) | copy-start | bytes 49156
  125.2 287.1 %copy-start.10 = (f32[4096]{0:T(1024)S(1)}, f32[4096]{0:T(1024)}, u32[]{:S(2)}) copy-start(f32[4096]{0:T(1024)} %param.21) | copy-start | bytes 49156
  125.3 287.1 %copy-start.11 = (f32[4096]{0:T(1024)S(1)}, f32[4096]{0:T(1024)}, u32[]{:S(2)}) copy-start(f32[4096]{0:T(1024)} %param.22) | copy-start | bytes 49156
  125.3 287.1 %copy-start.12 = (f32[4096]{0:T(1024)S(1)}, f32[4096]{0:T(1024)}, u32[]{:S(2)}) copy-start(f32[4096]{0:T(1024)} %param.23) | copy-start | bytes 49156
  125.3 287.1 %copy-start.13 = (f32[4096]{0:T(1024)S(1)}, f32[4096]{0:T(1024)}, u32[]{:S(2)}) copy-start(f32[4096]{0:T(1024)} %param.18) | copy-start | bytes 49156
  125.3 287.1 %copy-start.17 = (f32[4096]{0:T(1024)S(1)}, f32[4096]{0:T(1024)}, u32[]{:S(2)}) copy-start(f32[4096]{0:T(1024)} %param.19) | copy-start | bytes 49156
  127.3 285.0 %all-reduce.9.cloned.1.call-start = ((), (), s32[]{:S(2)}) async-start(), calls=%async_computation | async-start | bytes 262144
  129.2 542.2 %all-reduce.15.cloned.1.call-start = ((), (), s32[]{:S(2)}) async-start(), calls=%async_computation.3 | async-start | bytes 262144
  479.8 2.1 copy-start.4
  479.8 3.6 copy-start
  483.5 5.7 copy-start.5
  493.9 2.1 copy-start.4
  493.9 3.6 copy-start
  497.6 5.7 copy-start.5
  508.0 2.1 copy-start.4
  508.0 3.6 copy-start
  511.7 5.7 copy-start.5
  517.3 287.3 %copy-start.14 = (f32[4096]{0:T(1024)S(1)}, f32[4096]{0:T(1024)}, u32[]{:S(2)}) copy-start(f32[4096]{0:T(1024)} %get-tuple-element.347) | copy-start | bytes 49156
  517.3 287.3 %copy-start.15 = (f32[4096]{0:T(1024)S(1)}, f32[4096]{0:T(1024)}, u32[]{:S(2)}) copy-start(f32[4096]{0:T(1024)} %get-tuple-element.348) | copy-start | bytes 49156
  519.2 285.4 %all-reduce.13.cloned.1.call-start = ((), (), s32[]{:S(2)}) async-start(), calls=%async_computation.2 | async-start | bytes 262144
Sparse Core Ops, SparseCore 0:
  127.4 151.4 all-reduce.10
  281.5 130.7 all-reduce.8
  519.4 151.9 all-reduce.14
  673.8 130.7 all-reduce.12
where the time goes:
time: 814 us; the launch traced here: 813 us
  waiting for transfers between devices  564 us (69%)
  blocking collectives  124 us (15%)
  local copies, waits for them, and re-layouts  53.7 us (7%)
  other arithmetic  43.9 us (5%)
  between operations  15.9 us (2%)
  matrix products  10.9 us (1%)
    unnamed x8, waiting for transfers between devices  564 us
    all_gather x2, blocking collectives, on_device(): col_rates = lax.all_gather(pushed, 'row', axis=0, tiled=True)  72.5 us
    all_gather x2, blocking collectives, on_device(): row_rates = lax.all_gather(pushed, 'col', axis=0, tiled=True)  51.1 us
    scatter-add x12, other arithmetic, turn_body(): return (row_acc.at[row_slot].add(direct), col_acc.at[col_slot].add(mirror))  27.6 us
    reshape x6, local copies, waits for them, and re-layouts, turn_body(): lax.dynamic_slice_in_dim(kernel_tiles, begin_slot, group_size, 0)  21 us
  transfers between devices with their start and end apart: 4, of which 4 were waited for; matrix products, arithmetic and copies ran while one was open for 1% of the time, Pallas kernels for 0%

commit v1 on v0

v1 whole, which is shorter than its diff:
```python
import functools

import jax
import jax.numpy as jnp
from jax import lax
from jax.experimental import pallas as pl
from jax.experimental.pallas import tpu as pltpu
from jax.sharding import PartitionSpec as P

STEPS = 2
NEWTON = 4
TILE = 64
LANES = 128
CHUNK = 128

time_step = 0.25


def inverse_sinh(value):
    return jnp.log(value + jnp.sqrt(1.0 + value * value))


def friction_solve(rate_log, stress, state, normal_stress, rate_param, damping):
    strength = normal_stress * rate_param
    lift = state / rate_param
    for turn_index in range(NEWTON):
        speed = jnp.exp(rate_log)
        ratio = 0.5 * jnp.exp(rate_log + lift)
        root = jnp.sqrt(1.0 + ratio * ratio)
        misfit = stress - damping * speed - strength * jnp.log(ratio + root)
        slope = -damping * speed - strength * ratio / root
        rate_log = rate_log - misfit / slope
    return rate_log


def start_kernel(log_rate, state, excess, normal_stress, rate_param, damping, stress_out, pushed_out):
    speed = jnp.exp(log_rate[...])
    balance = normal_stress[...] * rate_param[...] * inverse_sinh(
        0.5 * jnp.exp(log_rate[...] + state[...] / rate_param[...])
    ) + damping[...] * speed
    stress_out[...] = balance * (1.0 + excess[...])
    pushed = (speed - 1.0).astype(jnp.bfloat16)
    pushed_out[...] = jnp.broadcast_to(pushed[None], pushed_out.shape)


def step_kernel(
    direct,
    mirror,
    rate_log,
    stress,
    state,
    normal_stress,
    rate_param,
    state_param,
    slip_length,
    self_stiffness,
    damping,
    rate_out,
    state_out,
    stress_out,
    *pushed_out,
):
    stress_rate = jnp.sum(direct[...].astype(jnp.float32), axis=0) + jnp.sum(
        mirror[...].astype(jnp.float32), axis=0
    )
    speed = jnp.exp(rate_log[...])
    old_state = state[...]
    new_stress = stress[...] + time_step * (stress_rate - self_stiffness[...] * (speed - 1.0))
    new_state = old_state + time_step * (state_param[...] / slip_length[...]) * (
        jnp.exp(-old_state / state_param[...]) - speed
    )
    new_rate = friction_solve(
        rate_log[...], new_stress, new_state, normal_stress[...], rate_param[...], damping[...]
    )
    rate_out[...] = new_rate
    state_out[...] = new_state
    stress_out[...] = new_stress
    for out in pushed_out:
        pushed = (jnp.exp(new_rate) - 1.0).astype(jnp.bfloat16)
        out[...] = jnp.broadcast_to(pushed[None], out.shape)


def pick_half(values, odd):
    lane = lax.broadcasted_iota(jnp.int32, values.shape, 1)
    return jnp.where((lane < TILE) == (odd == 0), values, pltpu.roll(values, TILE, 1))


def place_half(values, odd):
    lane = lax.broadcasted_iota(jnp.int32, values.shape, 1)
    return jnp.where((lane < TILE) == (odd == 0), values, 0.0)


def product_kernel(
    tiles, across, down, down_mirror, row_rates, col_rates, spread, gather, row_out, col_out, row_acc, col_acc
):
    chunk = pl.program_id(0)

    @pl.when(chunk == 0)
    def _():
        row_acc[...] = jnp.zeros_like(row_acc)
        col_acc[...] = jnp.zeros_like(col_acc)

    pairs = row_rates.shape[0]
    bf16 = jnp.bfloat16
    row_slot = across[:, 0:1]
    col_slot = across[:, 1:2]
    wide = lax.broadcasted_iota(jnp.int32, (CHUNK, pairs), 1)
    row_pick = jnp.where(wide == row_slot // 2, 1.0, 0.0).astype(bf16)
    col_pick = jnp.where(wide == col_slot // 2, 1.0, 0.0).astype(bf16)
    tall = lax.broadcasted_iota(jnp.int32, (pairs, CHUNK), 0)
    row_drop = jnp.where(tall == down[0:1, :], 1.0, 0.0).astype(bf16)
    col_drop = jnp.where(tall == down_mirror[0:1, :], 1.0, 0.0).astype(bf16)

    col_piece = jnp.dot(col_pick, col_rates[...], preferred_element_type=jnp.float32)
    row_piece = jnp.dot(row_pick, row_rates[...], preferred_element_type=jnp.float32)
    col_piece = pick_half(col_piece, col_slot % 2).astype(bf16)
    row_piece = pick_half(row_piece, row_slot % 2).astype(bf16)

    direct = jnp.zeros((CHUNK, LANES), jnp.float32)
    mirror = jnp.zeros((CHUNK, LANES), jnp.float32)
    width = 2 * LANES
    col_wide = jnp.concatenate([col_piece, col_piece], axis=1)
    for part in range(tiles.shape[1] // width):
        lanes = pl.ds(part * width, width)
        tile = tiles[:, lanes]
        direct += jnp.dot(tile * col_wide, gather[lanes, :], preferred_element_type=jnp.float32)
        spread_rate = jnp.dot(row_piece, spread[:, lanes], preferred_element_type=jnp.float32)
        product = tile.astype(jnp.float32) * spread_rate
        mirror += product[:, :LANES] + product[:, LANES:]
    mirror = mirror + pltpu.roll(mirror, TILE, 1)
    direct = place_half(direct, row_slot % 2).astype(bf16)
    mirror = place_half(mirror, col_slot % 2).astype(bf16)
    row_acc[...] += jnp.dot(row_drop, direct, preferred_element_type=jnp.float32)
    col_acc[...] += jnp.dot(col_drop, mirror, preferred_element_type=jnp.float32)

    @pl.when(chunk == pl.num_programs(0) - 1)
    def _():
        row_out[...] = row_acc[...].astype(bf16)
        col_out[...] = col_acc[...].astype(bf16)


def on_device(
    log_rate,
    state,
    excess,
    normal_stress,
    rate_param,
    state_param,
    slip_length,
    self_stiffness,
    damping,
    blocks,
    pattern,
    counts,
):
    patches = log_rate.shape[0]
    per_seg = patches // TILE
    my_row = lax.axis_index("row")
    my_col = lax.axis_index("col")
    row_count = lax.axis_size("row")
    col_count = lax.axis_size("col")
    slots = blocks.shape[2]
    tile_size = blocks.shape[3]
    flat = (patches // LANES, LANES)
    bf16 = jnp.bfloat16
    f32 = jnp.float32

    kernel_tiles = blocks.reshape(slots, tile_size)
    places = pattern.reshape(slots, 2)
    row_slot = places[:, 0]
    col_slot = places[:, 1]
    live = jnp.arange(slots, dtype=jnp.int32) < counts[0, 0]
    diagonal = (col_slot // per_seg == my_row) & (row_slot == my_col * per_seg + col_slot % per_seg)
    across = jnp.where(live[:, None], places, -2)
    down = jnp.where(live, row_slot // 2, -1)[None]
    down_mirror = jnp.where(live & jnp.logical_not(diagonal), col_slot // 2, -1)[None]
    entry = jnp.arange(tile_size, dtype=jnp.int32)
    lane = jnp.arange(LANES, dtype=jnp.int32)
    spread = (entry[None, :] // TILE == lane[:, None]).astype(bf16)
    gather = (entry[:, None] // TILE == lane[None, :] % TILE).astype(bf16)

    whole = [a.reshape(flat) for a in (normal_stress, rate_param, state_param, slip_length, self_stiffness, damping)]
    normal_stress, rate_param, state_param, slip_length, self_stiffness, damping = whole
    rate_log = log_rate.reshape(flat)
    state = state.reshape(flat)
    group = (row_count,) + flat

    stress, pushed = pl.pallas_call(
        start_kernel,
        out_shape=(jax.ShapeDtypeStruct(flat, f32), jax.ShapeDtypeStruct(group, bf16)),
    )(rate_log, state, excess.reshape(flat), normal_stress, rate_param, damping)

    def exchange(x, axis):
        return lax.all_to_all(x, axis, split_axis=0, concat_axis=0, tiled=True)

    row_pairs = col_count * per_seg // 2
    col_pairs = row_count * per_seg // 2
    product = pl.pallas_call(
        product_kernel,
        grid=(slots // CHUNK,),
        in_specs=[
            pl.BlockSpec((CHUNK, tile_size), lambda i: (i, 0)),
            pl.BlockSpec((CHUNK, 2), lambda i: (i, 0)),
            pl.BlockSpec((1, CHUNK), lambda i: (0, i)),
            pl.BlockSpec((1, CHUNK), lambda i: (0, i)),
            pl.BlockSpec((row_pairs, LANES), lambda i: (0, 0)),
            pl.BlockSpec((col_pairs, LANES), lambda i: (0, 0)),
            pl.BlockSpec((LANES, tile_size), lambda i: (0, 0)),
            pl.BlockSpec((tile_size, LANES), lambda i: (0, 0)),
        ],
        out_specs=[
            pl.BlockSpec((row_pairs, LANES), lambda i: (0, 0)),
            pl.BlockSpec((col_pairs, LANES), lambda i: (0, 0)),
        ],
        out_shape=(
            jax.ShapeDtypeStruct((row_pairs, LANES), bf16),
            jax.ShapeDtypeStruct((col_pairs, LANES), bf16),
        ),
        scratch_shapes=[pltpu.VMEM((row_pairs, LANES), f32), pltpu.VMEM((col_pairs, LANES), f32)],
    )
    for step_index in range(STEPS):
        last = step_index == STEPS - 1
        row_rates = exchange(pushed, "col")
        col_rates = exchange(pushed, "row")
        row_total, col_total = product(
            kernel_tiles,
            across,
            down,
            down_mirror,
            row_rates.reshape(row_pairs, LANES),
            col_rates.reshape(col_pairs, LANES),
            spread,
            gather,
        )
        direct = exchange(row_total.reshape((col_count,) + flat), "col")
        mirror = exchange(col_total.reshape((row_count,) + flat), "row")
        outs = [jax.ShapeDtypeStruct(flat, f32)] * 3
        if not last:
            outs.append(jax.ShapeDtypeStruct(group, bf16))
        result = pl.pallas_call(step_kernel, out_shape=tuple(outs))(
            direct,
            mirror,
            rate_log,
            stress,
            state,
            normal_stress,
            rate_param,
            state_param,
            slip_length,
            self_stiffness,
            damping,
        )
        rate_log, state, stress = result[:3]
        if not last:
            pushed = result[3]
    return tuple(a.reshape(patches) for a in (rate_log, state, stress))


def solution(mesh):
    in_specs = (P(("row", "col")),) * 9 + (
        P("row", "col", None, None),
        P("row", "col", None, None),
        P("row", "col"),
    )
    out_specs = (P(("row", "col")), P(("row", "col")), P(("row", "col")))
    return jax.shard_map(
        on_device, mesh=mesh, in_specs=in_specs, out_specs=out_specs, check_vma=False
    )
```

time: 814 us -> 133 us (0.16)
  waiting for transfers between devices: 564 us -> 8.09 us
  local copies, waits for them, and re-layouts: 53.7 us -> 1.79 us
  blocking collectives: 124 us -> 76.8 us
  other arithmetic: 43.9 us -> 5.34 us
  Pallas kernels: 0 us -> 20.9 us
  starting transfers between devices: 0.16 us -> 17.4 us
  between operations: 15.9 us -> 1.33 us
  matrix products: 10.9 us -> 0 us
    unnamed x8 -> x0, waiting for transfers between devices: 564 us -> none
    all_gather x4 -> x0, blocking collectives: 124 us -> none  [the longest x2 72.5 us: on_device(): col_rates = lax.all_gather(pushed, 'row', axis=0, tiled=True)]
    all_to_all x0 -> x6, blocking collectives: none -> 76.8 us  [exchange(): return lax.all_to_all(x, axis, split_axis=0, concat_axis=0, tiled=True)]
    scatter-add x12 -> x0, other arithmetic: 27.6 us -> none  [turn_body(): return (row_acc.at[row_slot].add(direct), col_acc.at[col_slot].add(mirror))]
    reshape x10 -> x0, local copies, waits for them, and re-layouts: 23 us -> none  [the longest x6 21 us: turn_body(): lax.dynamic_slice_in_dim(kernel_tiles, begin_slot, group_size, 0)]
    pallas_call x0 -> x5, Pallas kernels: none -> 20.9 us  [the longest x2 15.7 us: on_device(): product(kernel_tiles, across, down, down_mirror, row_rates.reshape(row_pa...]
    all_to_all x0 -> x2, starting transfers between devices: none -> 17.4 us  [exchange(): return lax.all_to_all(x, axis, split_axis=0, concat_axis=0, tiled=True)]
    dot_general x12 -> x0, matrix products: 10.9 us -> none  [the longest x6 7 us: turn_body(): jnp.einsum('bij,bi->bj', block_tiles, row_pieces[row_slot], preferred_ele...]
  transfers between devices with their start and end apart: 4 -> 2, of which waited for: 4 -> 1; matrix products, arithmetic and copies ran while one was open for 1% -> 5% of each run, Pallas kernels for 0% -> 0%
where the time goes in v1:
time: 133 us; the launch traced here: 132 us
  blocking collectives  76.8 us (58%)
  Pallas kernels  20.9 us (16%)
  starting transfers between devices  17.4 us (13%)
  waiting for transfers between devices  8.09 us (6%)
  other arithmetic  5.34 us (4%)
  local copies, waits for them, and re-layouts  1.79 us (1%)
  between operations  1.33 us (1%)
    all_to_all x6, blocking collectives, exchange(): return lax.all_to_all(x, axis, split_axis=0, concat_axis=0, tiled=True)  76.8 us
    all_to_all x2, starting transfers between devices, exchange(): return lax.all_to_all(x, axis, split_axis=0, concat_axis=0, tiled=True)  17.4 us
    pallas_call x2, Pallas kernels, on_device(): product(kernel_tiles, across, down, down_mirror, row_rates.reshape(row_pa...  15.7 us
    all_to_all x2, waiting for transfers between devices, exchange(): return lax.all_to_all(x, axis, split_axis=0, concat_axis=0, tiled=True)  8.09 us
    pallas_call x2, Pallas kernels, on_device(): pl.pallas_call(step_kernel, out_shape=tuple(outs))  3.76 us
    convert_element_type x1, other arithmetic, on_device(): gather = (entry[:, None] // TILE == lane[None, :] % TILE).astype(bf16)  2.68 us
  transfers between devices with their start and end apart: 2, of which 1 were waited for; matrix products, arithmetic and copies ran while one was open for 5% of the time, Pallas kernels for 0%

profile of v1, /device:TPU:1, one launch (start us, length us, event | category | flops | bytes accessed | tf_op | source)
XLA Modules:
  0.0 131.6 jit_solution(4736022246716511248)
XLA Ops:
  0.6 1.5 %shard_map.139 = (f32[32,128]{1,0:T(8,128)}, bf16[16,32,128]{2,1,0:T(8,128)(2,1)}) custom-call(f32[32,128]{1,0:T(8,128)} %bitcast.54, f32[32,128]{1,0:T(8,128)} %bitcast.56, f32[32,128]{1,0:T(8,128)} %bitcast.58, f32[32,128]{1,0:T(8,128)} %bitcast.35, f32[32,128]{1,0:T(8,128)} %bitcast.38, f32[32,128]{1,0:T(8,128)} %bitcast.41), custom_call_target="tpu_custom_call" | custom-call | tf_op jit(solution)/shard_map/pallas_call | solution.py:188
  2.1 6.9 %all-to-all-start = ((bf16[16,32,128]{2,1,0:T(8,128)(2,1)}), bf16[16,32,128]{2,1,0:T(8,128)(2,1)S(1)}, u32[]{:S(2)}, u32[]{:S(2)}) async-start(bf16[16,32,128]{2,1,0:T(8,128)(2,1)} %get-tuple-element.16), calls=%async_computation | async-start | bytes 262144 | tf_op jit(solution)/shard_map/all_to_all | solution.py:194
  9.7 0.8 copy.16
  10.5 0.3 slice_reduce_fusion
  10.8 1.2 fusion.spread
  12.0 2.7 %compare_convert_fusion.gather = bf16[4096,128]{1,0:T(8,128)(2,1)} fusion(s32[128]{0:T(128)S(1)} %and_select_fusion.5, s32[4096]{0:T(1024)S(1)} %add_select_fusion), kind=kLoop, calls=%fused_computation.2 | loop fusion | flops 1048576 | bytes 1065472 | tf_op jit(solution)/shard_map/convert_element_type | solution.py:180
  14.7 0.6 and_select_fusion.1
  15.3 0.0 all-to-all-done
  15.3 0.0 copy-start
  15.3 10.5 %all-to-all-start.1 = ((bf16[16,32,128]{2,1,0:T(8,128)(2,1)}), bf16[16,32,128]{2,1,0:T(8,128)(2,1)S(1)}, u32[]{:S(2)}, u32[]{:S(2)}) async-start(bf16[16,32,128]{2,1,0:T(8,128)(2,1)} %get-tuple-element.16), calls=%async_computation.1 | async-start | bytes 262144 | tf_op jit(solution)/shard_map/all_to_all | solution.py:194
  25.8 0.8 broadcast_select_fusion.across
  26.6 8.1 %all-to-all-done.1 = bf16[16,32,128]{2,1,0:T(8,128)(2,1)S(1)} async-done(((bf16[16,32,128]{2,1,0:T(8,128)(2,1)}), bf16[16,32,128]{2,1,0:T(8,128)(2,1)S(1)}, u32[]{:S(2)}, u32[]{:S(2)}) %all-to-all-start.1) | async-done | bytes 131104 | tf_op jit(solution)/shard_map/all_to_all | solution.py:194
  34.7 0.0 copy-start.1
  34.7 0.0 copy-done
  34.7 0.6 copy-done.1
  35.4 7.8 %shard_map.140 = (bf16[512,128]{1,0:T(8,128)(2,1)}, bf16[512,128]{1,0:T(8,128)(2,1)}) custom-call(bf16[512,4096]{1,0:T(8,128)(2,1)} %bitcast.28, s32[512,2]{1,0:T(8,128)} %broadcast_select_fusion.across, s32[1,512]{1,0:T(1,128)} %get-tuple-element.32.down, s32[1,512]{1,0:T(1,128)} %get-tuple-element.31.down_mirror, bf16[512,128]{1,0:T(8,128)(2,1)} %bitcast.31, ...), custom_call_target="tpu_custom_call" | custom-call | tf_op jit(solution)/shard_map/pallas_call | solution.py:225
  43.2 12.9 %all_to_all.40.direct = bf16[16,32,128]{2,1,0:T(8,128)(2,1)} all-to-all(bf16[16,32,128]{2,1,0:T(8,128)(2,1)} %bitcast.47), channel_id=1, replica_groups=mesh['row'=16,'col'=16] {'col'}, dimensions={0} | all-to-all | bytes 262144 | tf_op jit(solution)/shard_map/all_to_all | solution.py:194
  56.1 13.1 %all_to_all.41.mirror = bf16[16,32,128]{2,1,0:T(8,128)(2,1)} all-to-all(bf16[16,32,128]{2,1,0:T(8,128)(2,1)} %bitcast.46), channel_id=1, replica_groups=mesh['row'=16,'col'=16] {'row'}, dimensions={0} | all-to-all | bytes 262144 | tf_op jit(solution)/shard_map/all_to_all | solution.py:194
  69.2 1.9 %shard_map.141 = (f32[32,128]{1,0:T(8,128)}, f32[32,128]{1,0:T(8,128)}, f32[32,128]{1,0:T(8,128)}, bf16[16,32,128]{2,1,0:T(8,128)(2,1)}) custom-call(bf16[16,32,128]{2,1,0:T(8,128)(2,1)} %all_to_all.40.direct, bf16[16,32,128]{2,1,0:T(8,128)(2,1)} %all_to_all.41.mirror, f32[32,128]{1,0:T(8,128)} %bitcast.55, f32[32,128]{1,0:T(8,128)} %get-tuple-element.19.stress, ...), custom_call_target="tpu_custom_call" | custom-call | tf_op jit(solution)/shard_map/pallas_call | solution.py:240
  71.1 12.3 %all_to_all.42 = bf16[16,32,128]{2,1,0:T(8,128)(2,1)} all-to-all(bf16[16,32,128]{2,1,0:T(8,128)(2,1)} %get-tuple-element.20), channel_id=1, replica_groups=mesh['row'=16,'col'=16] {'col'}, dimensions={0} | all-to-all | bytes 262144 | tf_op jit(solution)/shard_map/all_to_all | solution.py:194
  83.4 13.1 %all_to_all.43 = bf16[16,32,128]{2,1,0:T(8,128)(2,1)} all-to-all(bf16[16,32,128]{2,1,0:T(8,128)(2,1)} %get-tuple-element.20), channel_id=1, replica_groups=mesh['row'=16,'col'=16] {'row'}, dimensions={0} | all-to-all | bytes 262144 | tf_op jit(solution)/shard_map/all_to_all | solution.py:194
  96.5 7.8 %shard_map.142 = (bf16[512,128]{1,0:T(8,128)(2,1)}, bf16[512,128]{1,0:T(8,128)(2,1)}) custom-call(bf16[512,4096]{1,0:T(8,128)(2,1)} %bitcast.29, s32[512,2]{1,0:T(8,128)} %broadcast_select_fusion.across, s32[1,512]{1,0:T(1,128)} %get-tuple-element.32.down, s32[1,512]{1,0:T(1,128)} %get-tuple-element.31.down_mirror, bf16[512,128]{1,0:T(8,128)(2,1)} %bitcast.33, ...), custom_call_target="tpu_custom_call" | custom-call | tf_op jit(solution)/shard_map/pallas_call | solution.py:225
  104.3 12.3 %all_to_all.44.direct = bf16[16,32,128]{2,1,0:T(8,128)(2,1)} all-to-all(bf16[16,32,128]{2,1,0:T(8,128)(2,1)} %bitcast.45), channel_id=1, replica_groups=mesh['row'=16,'col'=16] {'col'}, dimensions={0} | all-to-all | bytes 262144 | tf_op jit(solution)/shard_map/all_to_all | solution.py:194
  116.6 13.1 %all_to_all.45.mirror = bf16[16,32,128]{2,1,0:T(8,128)(2,1)} all-to-all(bf16[16,32,128]{2,1,0:T(8,128)(2,1)} %bitcast.44), channel_id=1, replica_groups=mesh['row'=16,'col'=16] {'row'}, dimensions={0} | all-to-all | bytes 262144 | tf_op jit(solution)/shard_map/all_to_all | solution.py:194
  129.7 1.9 %shard_map.143 = (f32[32,128]{1,0:T(8,128)}, f32[32,128]{1,0:T(8,128)}, f32[32,128]{1,0:T(8,128)}) custom-call(bf16[16,32,128]{2,1,0:T(8,128)(2,1)} %all_to_all.44.direct, bf16[16,32,128]{2,1,0:T(8,128)(2,1)} %all_to_all.45.mirror, f32[32,128]{1,0:T(8,128)} %get-tuple-element.23.rate_log, f32[32,128]{1,0:T(8,128)} %get-tuple-element.24.stress, ...), custom_call_target="tpu_custom_call" | custom-call | tf_op jit(solution)/shard_map/pallas_call | solution.py:240
  (3 shorter events, 0.0 us)
Async XLA Ops:
  2.1 13.2 %all-to-all-start = ((bf16[16,32,128]{2,1,0:T(8,128)(2,1)}), bf16[16,32,128]{2,1,0:T(8,128)(2,1)S(1)}, u32[]{:S(2)}, u32[]{:S(2)}) async-start(bf16[16,32,128]{2,1,0:T(8,128)(2,1)} %get-tuple-element.16), calls=%async_computation | async-start | bytes 262144 | tf_op jit(solution)/shard_map/all_to_all | solution.py:194
  15.3 19.4 %copy-start = (bf16[16,32,128]{2,1,0:T(8,128)(2,1)}, bf16[16,32,128]{2,1,0:T(8,128)(2,1)S(1)}, u32[]{:S(2)}) copy-start(bf16[16,32,128]{2,1,0:T(8,128)(2,1)S(1)} %all-to-all-done) | copy-start | bytes 393220
  15.3 19.4 %all-to-all-start.1 = ((bf16[16,32,128]{2,1,0:T(8,128)(2,1)}), bf16[16,32,128]{2,1,0:T(8,128)(2,1)S(1)}, u32[]{:S(2)}, u32[]{:S(2)}) async-start(bf16[16,32,128]{2,1,0:T(8,128)(2,1)} %get-tuple-element.16), calls=%async_computation.1 | async-start | bytes 262144 | tf_op jit(solution)/shard_map/all_to_all | solution.py:194
  34.7 0.7 copy-start.1

commit v2 on v0

v2 whole, which is shorter than its diff:
```python
import jax
import jax.numpy as jnp
from jax import lax
from jax.experimental import pallas as pl
from jax.experimental.pallas import tpu as pltpu
from jax.sharding import PartitionSpec as P

STEPS = 2
NEWTON = 4
TILE = 64
LANES = 128
WIDTH = 256
ROWS = 128

time_step = 0.25
bf16 = jnp.bfloat16
f32 = jnp.float32


def friction_solve(rate_log, stress, state, normal_stress, rate_param, damping):
    strength = normal_stress * rate_param
    lift = state / rate_param
    for turn_index in range(NEWTON):
        speed = jnp.exp(rate_log)
        ratio = 0.5 * jnp.exp(rate_log + lift)
        root = jnp.sqrt(1.0 + ratio * ratio)
        misfit = stress - damping * speed - strength * jnp.log(ratio + root)
        slope = -damping * speed - strength * ratio / root
        rate_log = rate_log - misfit / slope
    return rate_log


def push_kernel(log_rate, pushed_out):
    pushed = (jnp.exp(log_rate[...]) - 1.0).astype(bf16)
    pushed_out[...] = jnp.broadcast_to(pushed[None], pushed_out.shape)


def as_column(row):
    wide = jnp.broadcast_to(row.astype(f32), (LANES, row.shape[1]))
    return jnp.transpose(wide).astype(jnp.int32)


def plan_kernel(
    places, counts, row_pick, col_pick, row_drop, col_drop, row_half, col_half, spread, gather
):
    slots = places.shape[1]
    row_slot = places[0:1, :]
    col_slot = places[1:2, :]
    segment = row_drop.shape[0] * 2 // lax.axis_size("col")
    my_row = lax.axis_index("row")
    my_col = lax.axis_index("col")
    live = lax.broadcasted_iota(jnp.int32, (1, slots), 1) < counts[0, 0]
    diagonal = (col_slot // segment == my_row) & (row_slot == my_col * segment + col_slot % segment)
    row_live = jnp.where(live, row_slot, -2)
    col_live = jnp.where(live, col_slot, -2)
    col_twin = jnp.where(live & jnp.logical_not(diagonal), col_slot, -2)

    for drop, index in ((row_drop, row_live), (col_drop, col_twin)):
        tall = lax.broadcasted_iota(jnp.int32, drop.shape, 0)
        drop[...] = jnp.where(tall == (index >> 1), 1.0, 0.0).astype(bf16)
    for pick, half, index in ((row_pick, row_half, row_live), (col_pick, col_half, col_live)):
        column = as_column(index)
        pair = column >> 1
        lane = lax.broadcasted_iota(jnp.int32, column.shape, 1)
        for start in range(0, pick.shape[1], LANES):
            pick[:, start : start + LANES] = jnp.where(pair == lane + start, 1.0, 0.0).astype(bf16)
        half[...] = jnp.where((lane < TILE) == ((column & 1) == 0), 1.0, 0.0)
    entry = lax.broadcasted_iota(jnp.int32, spread.shape, 1)
    spread[...] = jnp.where(
        entry // TILE == lax.broadcasted_iota(jnp.int32, spread.shape, 0), 1.0, 0.0
    ).astype(bf16)
    entry = lax.broadcasted_iota(jnp.int32, gather.shape, 0)
    gather[...] = jnp.where(
        entry // TILE == lax.broadcasted_iota(jnp.int32, gather.shape, 1) % TILE, 1.0, 0.0
    ).astype(bf16)


def chosen(pick, half, rates):
    both = jnp.dot(pick, rates, preferred_element_type=f32)
    return jnp.where(half > 0.5, both, pltpu.roll(both, TILE, 1)).astype(bf16)


def mirror_kernel(tiles, pick, row_half, col_half, drop, spread, rates, pushed, out, parts):
    rates = rates[...].reshape(-1, LANES)
    for base in range(0, tiles.shape[0], ROWS):
        rows = slice(base, base + ROWS)
        piece = chosen(pick[rows, :], row_half[rows, :], rates)
        total = jnp.zeros((ROWS, LANES), f32)
        for start in range(0, tiles.shape[1], WIDTH):
            wide = jnp.dot(piece, spread[:, start : start + WIDTH], preferred_element_type=f32)
            product = tiles[rows, start : start + WIDTH].astype(f32) * wide
            total += product[:, :LANES] + product[:, LANES:]
        total = total + pltpu.roll(total, TILE, 1)
        parts[rows, :] = (total * col_half[rows, :]).astype(bf16)
    sums = jnp.dot(drop[...], parts[...], preferred_element_type=f32)
    patches = pushed.shape[1]
    out[:, :patches, :] = sums.astype(bf16).reshape(pushed.shape)
    out[:, patches:, :] = pushed[...]


def direct_kernel(tiles, pick, col_half, row_half, drop, gather, got, out, parts):
    patches = out.shape[1]
    rates = got[:, patches:, :].reshape(-1, LANES)
    for base in range(0, tiles.shape[0], ROWS):
        rows = slice(base, base + ROWS)
        piece = chosen(pick[rows, :], col_half[rows, :], rates)
        piece = jnp.concatenate([piece] * (WIDTH // LANES), axis=1)
        total = jnp.zeros((ROWS, LANES), f32)
        for start in range(0, tiles.shape[1], WIDTH):
            total += jnp.dot(
                tiles[rows, start : start + WIDTH] * piece,
                gather[start : start + WIDTH, :],
                preferred_element_type=f32,
            )
        parts[rows, :] = (total * row_half[rows, :]).astype(bf16)
    sums = jnp.dot(drop[...], parts[...], preferred_element_type=f32)
    out[...] = sums.astype(bf16).reshape(out.shape)


def step_body(stress, direct, got, rate_log, state, more, outs):
    normal_stress, rate_param, state_param, slip_length, self_stiffness, damping = (m[...] for m in more)
    rate_out, state_out, stress_out, *pushed_out = outs
    stress_rate = jnp.sum(direct[...].astype(f32), axis=0) + jnp.sum(
        got[:, : direct.shape[1], :].astype(f32), axis=0
    )
    speed = jnp.exp(rate_log)
    new_stress = stress + time_step * (stress_rate - self_stiffness * (speed - 1.0))
    new_state = state + time_step * (state_param / slip_length) * (jnp.exp(-state / state_param) - speed)
    new_rate = friction_solve(rate_log, new_stress, new_state, normal_stress, rate_param, damping)
    rate_out[...] = new_rate
    state_out[...] = new_state
    stress_out[...] = new_stress
    for out in pushed_out:
        pushed = (jnp.exp(new_rate) - 1.0).astype(bf16)
        out[...] = jnp.broadcast_to(pushed[None], out.shape)


def first_kernel(direct, got, log_rate, state, excess, *refs):
    more, outs = refs[:6], refs[6:]
    normal_stress, rate_param, damping = more[0][...], more[1][...], more[5][...]
    rate_log, begin = log_rate[...], state[...]
    ratio = 0.5 * jnp.exp(rate_log + begin / rate_param)
    balance = normal_stress * rate_param * jnp.log(ratio + jnp.sqrt(1.0 + ratio * ratio)) + damping * jnp.exp(
        rate_log
    )
    step_body(balance * (1.0 + excess[...]), direct, got, rate_log, begin, more, outs)


def later_kernel(direct, got, rate_log, state, stress, *refs):
    step_body(stress[...], direct, got, rate_log[...], state[...], refs[:6], refs[6:])


def call(kernel, out_shape, scratch=(), **kw):
    return pl.pallas_call(
        kernel,
        out_shape=out_shape,
        scratch_shapes=list(scratch),
        compiler_params=pltpu.CompilerParams(vmem_limit_bytes=24 << 20),
        **kw,
    )


def on_device(
    log_rate,
    state,
    excess,
    normal_stress,
    rate_param,
    state_param,
    slip_length,
    self_stiffness,
    damping,
    blocks,
    pattern,
    counts,
):
    patches = log_rate.shape[0]
    flat = (patches // LANES, LANES)
    row_count = lax.axis_size("row")
    col_count = lax.axis_size("col")
    slots, tile_size = blocks.shape[2:]
    row_rows = col_count * flat[0]
    col_rows = row_count * flat[0]
    shape = jax.ShapeDtypeStruct

    tiles = blocks.reshape(slots, tile_size)
    places = pattern.reshape(slots, 2).T
    more = [
        a.reshape(flat)
        for a in (normal_stress, rate_param, state_param, slip_length, self_stiffness, damping)
    ]
    rate_log = log_rate.reshape(flat)
    state = state.reshape(flat)
    stress = excess.reshape(flat)
    vmem = pl.BlockSpec(memory_space=pltpu.VMEM)

    def exchange(x, axis):
        return lax.all_to_all(x, axis, split_axis=0, concat_axis=0, tiled=True)

    pushed = call(push_kernel, shape((col_count,) + flat, bf16))(rate_log)
    row_pick, col_pick, row_drop, col_drop, row_half, col_half, spread, gather = call(
        plan_kernel,
        (
            shape((slots, row_rows), bf16),
            shape((slots, col_rows), bf16),
            shape((row_rows, slots), bf16),
            shape((col_rows, slots), bf16),
            shape((slots, LANES), f32),
            shape((slots, LANES), f32),
            shape((LANES, tile_size), bf16),
            shape((tile_size, LANES), bf16),
        ),
        in_specs=[vmem, pl.BlockSpec(memory_space=pltpu.SMEM)],
    )(places, counts)
    parts = (pltpu.VMEM((slots, LANES), bf16),)
    for step_index in range(STEPS):
        row_rates = exchange(pushed, "col")
        mixed = call(mirror_kernel, shape((row_count, 2 * flat[0], LANES), bf16), parts)(
            tiles, row_pick, row_half, col_half, col_drop, spread, row_rates, pushed
        )
        got = exchange(mixed, "row")
        direct = call(direct_kernel, shape((col_count,) + flat, bf16), parts)(
            tiles, col_pick, col_half, row_half, row_drop, gather, got
        )
        direct = exchange(direct, "col")
        outs = [shape(flat, f32)] * 3
        if step_index < STEPS - 1:
            outs.append(shape((col_count,) + flat, bf16))
        result = call(later_kernel if step_index else first_kernel, tuple(outs))(
            direct, got, rate_log, state, stress, *more
        )
        rate_log, state, stress = result[:3]
        pushed = result[-1]
    return tuple(a.reshape(patches) for a in (rate_log, state, stress))


def solution(mesh):
    in_specs = (P(("row", "col")),) * 9 + (
        P("row", "col", None, None),
        P("row", "col", None, None),
        P("row", "col"),
    )
    out_specs = (P(("row", "col")), P(("row", "col")), P(("row", "col")))
    return jax.shard_map(
        on_device, mesh=mesh, in_specs=in_specs, out_specs=out_specs, check_vma=False
    )
```

time: 814 us -> 98.3 us (0.12)
  waiting for transfers between devices: 564 us -> 1.1 us
  blocking collectives: 124 us -> 67.6 us
  local copies, waits for them, and re-layouts: 53.7 us -> 7.09 us
  other arithmetic: 43.9 us -> 0 us
  between operations: 15.9 us -> 1.48 us
  Pallas kernels: 0 us -> 13.6 us
  matrix products: 10.9 us -> 0 us
    unnamed x8 -> x0, waiting for transfers between devices: 564 us -> none
    all_gather x4 -> x0, blocking collectives: 124 us -> none  [the longest x2 72.5 us: on_device(): col_rates = lax.all_gather(pushed, 'row', axis=0, tiled=True)]
    all_to_all x0 -> x5, blocking collectives: none -> 67.6 us  [exchange(): return lax.all_to_all(x, axis, split_axis=0, concat_axis=0, tiled=True)]
    scatter-add x12 -> x0, other arithmetic: 27.6 us -> none  [turn_body(): return (row_acc.at[row_slot].add(direct), col_acc.at[col_slot].add(mirror))]
    reshape x10 -> x0, local copies, waits for them, and re-layouts: 23 us -> none  [the longest x6 21 us: turn_body(): lax.dynamic_slice_in_dim(kernel_tiles, begin_slot, group_size, 0)]
    pallas_call x0 -> x8, Pallas kernels: none -> 13.6 us  [the longest x2 5.95 us: on_device(): call(mirror_kernel, shape((row_count, 2 * flat[0], LANES), bf16), parts)]
    dot_general x12 -> x0, matrix products: 10.9 us -> none  [the longest x6 7 us: turn_body(): jnp.einsum('bij,bi->bj', block_tiles, row_pieces[row_slot], preferred_ele...]
    gather x12 -> x0, local copies, waits for them, and re-layouts: 8.53 us -> none  [the longest x6 4.27 us: turn_body(): col_pieces[col_slot]]
  transfers between devices with their start and end apart: 4 -> 1, of which waited for: 4 -> 1; matrix products, arithmetic and copies ran while one was open for 1% -> 0% of each run, Pallas kernels for 0% -> 1%
where the time goes in v2:
time: 98.3 us; the launch traced here: 97.8 us
  blocking collectives  67.6 us (69%)
  Pallas kernels  13.6 us (14%)
  local copies, waits for them, and re-layouts  7.09 us (7%)
  starting transfers between devices  6.9 us (7%)
  between operations  1.48 us (2%)
  waiting for transfers between devices  1.1 us (1%)
    all_to_all x5, blocking collectives, exchange(): return lax.all_to_all(x, axis, split_axis=0, concat_axis=0, tiled=True)  67.6 us
    unnamed x40, local copies, waits for them, and re-layouts  7.09 us
    all_to_all x1, starting transfers between devices, exchange(): return lax.all_to_all(x, axis, split_axis=0, concat_axis=0, tiled=True)  6.9 us
    pallas_call x2, Pallas kernels, on_device(): call(mirror_kernel, shape((row_count, 2 * flat[0], LANES), bf16), parts)  5.95 us
    pallas_call x2, Pallas kernels, on_device(): call(direct_kernel, shape((col_count,) + flat, bf16), parts)  4.71 us
  transfers between devices with their start and end apart: 1, of which 1 were waited for; matrix products, arithmetic and copies ran while one was open for 0% of the time, Pallas kernels for 1%

profile of v2, /device:TPU:1, one launch (start us, length us, event | category | flops | bytes accessed | tf_op | source)
XLA Modules:
  0.0 97.8 jit_solution(10752780403103281890)
XLA Ops:
  0.6 0.0 copy-start.9
  0.6 0.7 copy-done.9
  1.4 0.7 shard_map.140.pushed
  2.0 6.9 %all-to-all-start = ((bf16[16,32,128]{2,1,0:T(8,128)(2,1)}), bf16[16,32,128]{2,1,0:T(8,128)(2,1)S(1)}, u32[]{:S(2)}, u32[]{:S(2)}) async-start(bf16[16,32,128]{2,1,0:T(8,128)(2,1)} %shard_map.140.pushed), calls=%async_computation | async-start | bytes 262144 | tf_op jit(solution)/shard_map/all_to_all | solution.py:198
  9.6 0.0 copy-start.19
  9.6 0.7 copy-done.19
  10.3 1.2 %shard_map.139 = (bf16[512,512]{1,0:T(8,128)(2,1)S(1)}, bf16[512,512]{1,0:T(8,128)(2,1)S(1)}, bf16[512,512]{1,0:T(8,128)(2,1)S(1)}, bf16[512,512]{1,0:T(8,128)(2...) custom-call(s32[2,512]{1,0:T(2,128)S(1)} %bitcast.36, ...), custom_call_target="tpu_custom_call" | custom-call | tf_op jit(solution)/shard_map/pallas_call | solution.py:201
  11.5 0.0 copy-start.2
  11.5 0.8 copy-done.2
  12.3 0.0 copy-start.5
  12.3 0.8 copy-done.5
  13.1 0.0 copy-start.7
  13.1 0.8 copy-done.7
  13.9 1.1 %all-to-all-done.rates = bf16[16,32,128]{2,1,0:T(8,128)(2,1)S(1)} async-done(((bf16[16,32,128]{2,1,0:T(8,128)(2,1)}), bf16[16,32,128]{2,1,0:T(8,128)(2,1)S(1)}, u32[]{:S(2)}, u32[]{:S(2)}) %all-to-all-start) | async-done | bytes 131104 | tf_op jit(solution)/shard_map/all_to_all | solution.py:198
  15.0 0.0 copy-start
  15.0 2.2 %copy-done = bf16[1,1,512,4096]{3,2,1,0:T(8,128)(2,1)S(1)} copy-done((bf16[1,1,512,4096]{3,2,1,0:T(8,128)(2,1)S(1)}, bf16[1,1,512,4096]{3,2,1,0:T(8,128)(2,1)}, u32[]{:S(2)}) %copy-start) | copy-done | bytes 4194328
  17.2 0.0 copy-start.3
  17.2 1.0 %copy-done.3 = bf16[512,512]{1,0:T(8,128)(2,1)S(1)} copy-done((bf16[512,512]{1,0:T(8,128)(2,1)S(1)}, bf16[512,512]{1,0:T(8,128)(2,1)}, u32[]{:S(2)}) %copy-start.3) | copy-done | bytes 524312
  18.3 0.0 copy-start.1
  18.3 0.0 copy-start.6
  18.3 0.0 copy-start.8
  18.3 3.5 %shard_map.141 = bf16[16,64,128]{2,1,0:T(8,128)(2,1)S(1)} custom-call(bf16[512,4096]{1,0:T(8,128)(2,1)S(1)} %bitcast.16, bf16[512,512]{1,0:T(8,128)(2,1)S(1)} %get-tuple-element.23.pick, f32[512,128]{1,0:T(8,128)S(1)} %get-tuple-element.20.row_half, f32[512,128]{1,0:T(8,128)S(1)} %get-tuple-element.19.col_half, bf16[512,512]{1,0:T(8,128)(2,1)S(1)} %copy-done.3, ...), custom_call_target="tpu_custom_call" | custom-call | tf_op jit(solution)/shard_map/pallas_call | solution.py:218
  21.8 0.0 copy-start.10
  21.8 0.0 copy-start.11
  21.8 0.0 copy-start.12
  21.8 0.0 copy-start.13
  21.8 0.0 copy-start.14
  21.8 0.0 copy-start.15
  21.9 0.0 copy-start.16
  21.9 0.0 copy-start.17
  21.9 0.0 copy-start.18
  21.9 20.7 %all_to_all.30.got = bf16[16,64,128]{2,1,0:T(8,128)(2,1)S(1)} all-to-all(bf16[16,64,128]{2,1,0:T(8,128)(2,1)S(1)} %shard_map.141), channel_id=1, replica_groups=mesh['row'=16,'col'=16] {'row'}, dimensions={0} | all-to-all | bytes 524288 | tf_op jit(solution)/shard_map/all_to_all | solution.py:198
  42.6 0.0 copy-start.4
  42.6 0.0 copy-done.1
  42.6 0.0 copy-done.6
  42.6 0.0 copy-done.8
  42.6 2.4 %shard_map.142 = bf16[16,32,128]{2,1,0:T(8,128)(2,1)S(1)} custom-call(bf16[512,4096]{1,0:T(8,128)(2,1)S(1)} %bitcast.17, bf16[512,512]{1,0:T(8,128)(2,1)S(1)} %copy-done.6, f32[512,128]{1,0:T(8,128)S(1)} %get-tuple-element.19.col_half, f32[512,128]{1,0:T(8,128)S(1)} %get-tuple-element.20.row_half, bf16[512,512]{1,0:T(8,128)(2,1)S(1)} %copy-done.8, ...), custom_call_target="tpu_custom_call" | custom-call | tf_op jit(solution)/shard_map/pallas_call | solution.py:222
  44.9 11.9 %all_to_all.31.direct = bf16[16,32,128]{2,1,0:T(8,128)(2,1)S(1)} all-to-all(bf16[16,32,128]{2,1,0:T(8,128)(2,1)S(1)} %shard_map.142), channel_id=1, replica_groups=mesh['row'=16,'col'=16] {'col'}, dimensions={0} | all-to-all | bytes 262144 | tf_op jit(solution)/shard_map/all_to_all | solution.py:198
  56.8 0.0 copy-done.10
  56.8 0.0 copy-done.11
  56.8 0.0 copy-done.12
  56.8 0.0 copy-done.13
  56.8 0.0 copy-done.14
  56.8 0.0 copy-done.15
  56.8 0.0 copy-done.16
  56.8 0.0 copy-done.17
  56.9 0.0 copy-done.18
  56.9 0.2 shard_map.143
  57.1 9.3 %all_to_all.32.rates = bf16[16,32,128]{2,1,0:T(8,128)(2,1)S(1)} all-to-all(bf16[16,32,128]{2,1,0:T(8,128)(2,1)S(1)} %get-tuple-element.26.pushed), channel_id=1, replica_groups=mesh['row'=16,'col'=16] {'col'}, dimensions={0} | all-to-all | bytes 262144 | tf_op jit(solution)/shard_map/all_to_all | solution.py:198
  66.4 0.0 copy-done.4
  66.4 2.5 %shard_map.144 = bf16[16,64,128]{2,1,0:T(8,128)(2,1)S(1)} custom-call(bf16[512,4096]{1,0:T(8,128)(2,1)S(1)} %bitcast.18, bf16[512,512]{1,0:T(8,128)(2,1)S(1)} %get-tuple-element.23.pick, f32[512,128]{1,0:T(8,128)S(1)} %get-tuple-element.20.row_half, f32[512,128]{1,0:T(8,128)S(1)} %get-tuple-element.19.col_half, bf16[512,512]{1,0:T(8,128)(2,1)S(1)} %copy-done.4, ...), custom_call_target="tpu_custom_call" | custom-call | tf_op jit(solution)/shard_map/pallas_call | solution.py:218
  68.8 14.9 %all_to_all.33.got = bf16[16,64,128]{2,1,0:T(8,128)(2,1)S(1)} all-to-all(bf16[16,64,128]{2,1,0:T(8,128)(2,1)S(1)} %shard_map.144), channel_id=1, replica_groups=mesh['row'=16,'col'=16] {'row'}, dimensions={0} | all-to-all | bytes 524288 | tf_op jit(solution)/shard_map/all_to_all | solution.py:198
  83.7 2.4 %shard_map.145 = bf16[16,32,128]{2,1,0:T(8,128)(2,1)S(1)} custom-call(bf16[512,4096]{1,0:T(8,128)(2,1)S(1)} %bitcast.19, bf16[512,512]{1,0:T(8,128)(2,1)S(1)} %copy-done.6, f32[512,128]{1,0:T(8,128)S(1)} %get-tuple-element.19.col_half, f32[512,128]{1,0:T(8,128)S(1)} %get-tuple-element.20.row_half, bf16[512,512]{1,0:T(8,128)(2,1)S(1)} %copy-done.8, ...), custom_call_target="tpu_custom_call" | custom-call | tf_op jit(solution)/shard_map/pallas_call | solution.py:222
  86.1 10.9 %all_to_all.34.direct = bf16[16,32,128]{2,1,0:T(8,128)(2,1)S(1)} all-to-all(bf16[16,32,128]{2,1,0:T(8,128)(2,1)S(1)} %shard_map.145), channel_id=1, replica_groups=mesh['row'=16,'col'=16] {'col'}, dimensions={0} | all-to-all | bytes 262144 | tf_op jit(solution)/shard_map/all_to_all | solution.py:198
  97.0 0.8 shard_map.146
Async XLA Ops:
  0.6 0.7 copy-start.9
  2.0 13.0 %all-to-all-start = ((bf16[16,32,128]{2,1,0:T(8,128)(2,1)}), bf16[16,32,128]{2,1,0:T(8,128)(2,1)S(1)}, u32[]{:S(2)}, u32[]{:S(2)}) async-start(bf16[16,32,128]{2,1,0:T(8,128)(2,1)} %shard_map.140.pushed), calls=%async_computation | async-start | bytes 262144 | tf_op jit(solution)/shard_map/all_to_all | solution.py:198
  9.6 0.7 copy-start.19
  11.5 0.8 copy-start.2
  12.3 0.8 copy-start.5
  13.1 0.8 copy-start.7
  15.0 2.2 %copy-start = (bf16[1,1,512,4096]{3,2,1,0:T(8,128)(2,1)S(1)}, bf16[1,1,512,4096]{3,2,1,0:T(8,128)(2,1)}, u32[]{:S(2)}) copy-start(bf16[1,1,512,4096]{3,2,1,0:T(8,128)(2,1)} %param.21) | copy-start | bytes 12582916
  17.2 1.0 %copy-start.3 = (bf16[512,512]{1,0:T(8,128)(2,1)S(1)}, bf16[512,512]{1,0:T(8,128)(2,1)}, u32[]{:S(2)}) copy-start(bf16[512,512]{1,0:T(8,128)(2,1)} %copy-done.2) | copy-start | bytes 1572868
  18.3 24.3 %copy-start.1 = (bf16[1,1,512,4096]{3,2,1,0:T(8,128)(2,1)S(1)}, bf16[1,1,512,4096]{3,2,1,0:T(8,128)(2,1)}, u32[]{:S(2)}) copy-start(bf16[1,1,512,4096]{3,2,1,0:T(8,128)(2,1)} %param.21) | copy-start | bytes 12582916
  18.3 24.3 %copy-start.6 = (bf16[512,512]{1,0:T(8,128)(2,1)S(1)}, bf16[512,512]{1,0:T(8,128)(2,1)}, u32[]{:S(2)}) copy-start(bf16[512,512]{1,0:T(8,128)(2,1)} %copy-done.5) | copy-start | bytes 1572868
  18.3 24.3 %copy-start.8 = (bf16[512,512]{1,0:T(8,128)(2,1)S(1)}, bf16[512,512]{1,0:T(8,128)(2,1)}, u32[]{:S(2)}) copy-start(bf16[512,512]{1,0:T(8,128)(2,1)} %copy-done.7) | copy-start | bytes 1572868
  21.8 35.0 %copy-start.10 = (f32[4096]{0:T(1024)S(1)}, f32[4096]{0:T(1024)}, u32[]{:S(2)}) copy-start(f32[4096]{0:T(1024)} %param.12) | copy-start | bytes 49156
  21.8 35.0 %copy-start.11 = (f32[4096]{0:T(1024)S(1)}, f32[4096]{0:T(1024)}, u32[]{:S(2)}) copy-start(f32[4096]{0:T(1024)} %param.15) | copy-start | bytes 49156
  21.8 35.0 %copy-start.12 = (f32[4096]{0:T(1024)S(1)}, f32[4096]{0:T(1024)}, u32[]{:S(2)}) copy-start(f32[4096]{0:T(1024)} %param.16) | copy-start | bytes 49156
  21.8 35.0 %copy-start.13 = (f32[4096]{0:T(1024)S(1)}, f32[4096]{0:T(1024)}, u32[]{:S(2)}) copy-start(f32[4096]{0:T(1024)} %param.17) | copy-start | bytes 49156
  21.8 35.0 %copy-start.14 = (f32[4096]{0:T(1024)S(1)}, f32[4096]{0:T(1024)}, u32[]{:S(2)}) copy-start(f32[4096]{0:T(1024)} %param.18) | copy-start | bytes 49156
  21.8 35.0 %copy-start.15 = (f32[4096]{0:T(1024)S(1)}, f32[4096]{0:T(1024)}, u32[]{:S(2)}) copy-start(f32[4096]{0:T(1024)} %param.19) | copy-start | bytes 49156
  21.9 35.0 %copy-start.16 = (f32[4096]{0:T(1024)S(1)}, f32[4096]{0:T(1024)}, u32[]{:S(2)}) copy-start(f32[4096]{0:T(1024)} %param.20) | copy-start | bytes 49156
  21.9 35.0 %copy-start.17 = (f32[4096]{0:T(1024)S(1)}, f32[4096]{0:T(1024)}, u32[]{:S(2)}) copy-start(f32[4096]{0:T(1024)} %param.13) | copy-start | bytes 49156
  21.9 35.0 %copy-start.18 = (f32[4096]{0:T(1024)S(1)}, f32[4096]{0:T(1024)}, u32[]{:S(2)}) copy-start(f32[4096]{0:T(1024)} %param.14) | copy-start | bytes 49156
  42.6 23.8 %copy-start.4 = (bf16[512,512]{1,0:T(8,128)(2,1)S(1)}, bf16[512,512]{1,0:T(8,128)(2,1)}, u32[]{:S(2)}) copy-start(bf16[512,512]{1,0:T(8,128)(2,1)} %copy-done.2) | copy-start | bytes 1572868

commit v3 on v2

v3 whole, which is shorter than its diff:
```python
import jax
import jax.numpy as jnp
from jax import lax
from jax.experimental import pallas as pl
from jax.experimental.pallas import tpu as pltpu
from jax.sharding import PartitionSpec as P

STEPS = 2
NEWTON = 4
TILE = 64
LANES = 128
WIDTH = 256
ROWS = 128

time_step = 0.25
bf16 = jnp.bfloat16
f32 = jnp.float32


def friction_solve(rate_log, stress, state, normal_stress, rate_param, damping):
    strength = normal_stress * rate_param
    lift = state / rate_param
    for turn_index in range(NEWTON):
        speed = jnp.exp(rate_log)
        ratio = 0.5 * jnp.exp(rate_log + lift)
        root = jnp.sqrt(1.0 + ratio * ratio)
        misfit = stress - damping * speed - strength * jnp.log(ratio + root)
        slope = -damping * speed - strength * ratio / root
        rate_log = rate_log - misfit / slope
    return rate_log


def as_column(row):
    wide = jnp.broadcast_to(row.astype(f32), (LANES, row.shape[1]))
    return jnp.transpose(wide).astype(jnp.int32)


def push_kernel(log_rate_far, places_far, counts, pushed_out, index_out, log_rate, places, sems):
    copies = [
        pltpu.make_async_copy(log_rate_far, log_rate, sems.at[0]),
        pltpu.make_async_copy(places_far, places, sems.at[1]),
    ]
    for copy in copies:
        copy.start()
    for copy in copies:
        copy.wait()
    pushed = (jnp.exp(log_rate[...]) - 1.0).astype(bf16)
    pushed_out[...] = jnp.broadcast_to(pushed[None], pushed_out.shape)
    segment = log_rate.size // TILE
    row_slot, col_slot = places[0:1, :], places[1:2, :]
    live = lax.broadcasted_iota(jnp.int32, row_slot.shape, 1) < counts[0, 0]
    own = col_slot // segment == lax.axis_index("row")
    own = own & (row_slot == lax.axis_index("col") * segment + col_slot % segment)
    index_out[0:1, :] = jnp.where(live, row_slot, -2)
    index_out[1:2, :] = jnp.where(live, col_slot, -2)
    index_out[2:3, :] = jnp.where(live & jnp.logical_not(own), col_slot, -2)


def lower_half(column):
    lane = lax.broadcasted_iota(jnp.int32, column.shape, 1)
    return (lane < TILE) == ((column & 1) == 0)


def chosen(column, rates):
    lane = lax.broadcasted_iota(jnp.int32, column.shape, 1)
    pair = column >> 1
    pick = [
        jnp.where(pair == lane + start, 1.0, 0.0).astype(bf16)
        for start in range(0, rates.shape[0], LANES)
    ]
    both = jnp.dot(jnp.concatenate(pick, axis=1), rates, preferred_element_type=f32)
    return jnp.where(lower_half(column), both, pltpu.roll(both, TILE, 1)).astype(bf16)


def dropped(index, parts, rows):
    tall = lax.broadcasted_iota(jnp.int32, (rows, index.shape[1]), 0)
    drop = jnp.where(tall == (index >> 1), 1.0, 0.0).astype(bf16)
    return jnp.dot(drop, parts, preferred_element_type=f32).astype(bf16)


def fetch(tiles_far, tiles, sems):
    copies = []
    for turn, base in enumerate(range(0, tiles.shape[0], ROWS)):
        rows = pl.ds(base, ROWS)
        copies.append(pltpu.make_async_copy(tiles_far.at[rows, :], tiles.at[rows, :], sems.at[turn]))
        copies[-1].start()
    return copies


def mirror_kernel(tiles, index, rates, pushed, out, spread, parts, *near):
    copies = []
    if near:
        copies = fetch(tiles, *near)
        tiles = near[0]
    entry = lax.broadcasted_iota(jnp.int32, spread.shape, 1) // TILE
    spread[...] = jnp.where(
        entry == lax.broadcasted_iota(jnp.int32, spread.shape, 0), 1.0, 0.0
    ).astype(bf16)
    rates = rates[...].reshape(-1, LANES)
    row_index = index[0:1, :]
    col_index = index[1:2, :]
    for base in range(0, tiles.shape[0], ROWS):
        rows = slice(base, base + ROWS)
        piece = chosen(as_column(row_index[:, rows]), rates)
        if copies:
            copies[base // ROWS].wait()
        total = jnp.zeros((ROWS, LANES), f32)
        for start in range(0, tiles.shape[1], WIDTH):
            wide = jnp.dot(piece, spread[:, start : start + WIDTH], preferred_element_type=f32)
            product = tiles[rows, start : start + WIDTH].astype(f32) * wide
            total += product[:, :LANES] + product[:, LANES:]
        total = total + pltpu.roll(total, TILE, 1)
        half = lower_half(as_column(col_index[:, rows]))
        parts[rows, :] = jnp.where(half, total, 0.0).astype(bf16)
    patches = pushed.shape[1]
    sums = dropped(index[2:3, :], parts[...], pushed.shape[0] * patches)
    out[:, :patches, :] = sums.reshape(pushed.shape)
    out[:, patches:, :] = pushed[...]


def direct_kernel(tiles, index, got, out, gather, parts):
    entry = lax.broadcasted_iota(jnp.int32, gather.shape, 0) // TILE
    gather[...] = jnp.where(
        entry == lax.broadcasted_iota(jnp.int32, gather.shape, 1) % TILE, 1.0, 0.0
    ).astype(bf16)
    patches = out.shape[1]
    rates = got[:, patches:, :].reshape(-1, LANES)
    row_index = index[0:1, :]
    col_index = index[1:2, :]
    for base in range(0, tiles.shape[0], ROWS):
        rows = slice(base, base + ROWS)
        piece = chosen(as_column(col_index[:, rows]), rates)
        piece = jnp.concatenate([piece] * (WIDTH // LANES), axis=1)
        total = jnp.zeros((ROWS, LANES), f32)
        for start in range(0, tiles.shape[1], WIDTH):
            total += jnp.dot(
                tiles[rows, start : start + WIDTH] * piece,
                gather[start : start + WIDTH, :],
                preferred_element_type=f32,
            )
        half = lower_half(as_column(row_index[:, rows]))
        parts[rows, :] = jnp.where(half, total, 0.0).astype(bf16)
    sums = dropped(row_index, parts[...], out.shape[0] * patches)
    out[...] = sums.reshape(out.shape)


def step_body(stress, direct, got, rate_log, state, more, outs):
    normal_stress, rate_param, state_param, slip_length, self_stiffness, damping = (m[...] for m in more)
    rate_out, state_out, stress_out, *pushed_out = outs
    stress_rate = jnp.sum(direct[...].astype(f32), axis=0) + jnp.sum(
        got[:, : direct.shape[1], :].astype(f32), axis=0
    )
    speed = jnp.exp(rate_log)
    new_stress = stress + time_step * (stress_rate - self_stiffness * (speed - 1.0))
    new_state = state + time_step * (state_param / slip_length) * (jnp.exp(-state / state_param) - speed)
    new_rate = friction_solve(rate_log, new_stress, new_state, normal_stress, rate_param, damping)
    rate_out[...] = new_rate
    state_out[...] = new_state
    stress_out[...] = new_stress
    for out in pushed_out:
        pushed = (jnp.exp(new_rate) - 1.0).astype(bf16)
        out[...] = jnp.broadcast_to(pushed[None], out.shape)


def first_kernel(direct, got, log_rate, state, excess, *refs):
    more, outs = refs[:6], refs[6:]
    normal_stress, rate_param, damping = more[0][...], more[1][...], more[5][...]
    rate_log, begin = log_rate[...], state[...]
    ratio = 0.5 * jnp.exp(rate_log + begin / rate_param)
    balance = normal_stress * rate_param * jnp.log(ratio + jnp.sqrt(1.0 + ratio * ratio)) + damping * jnp.exp(
        rate_log
    )
    step_body(balance * (1.0 + excess[...]), direct, got, rate_log, begin, more, outs)


def later_kernel(direct, got, rate_log, state, stress, *refs):
    step_body(stress[...], direct, got, rate_log[...], state[...], refs[:6], refs[6:])


def call(kernel, out_shape, scratch=(), **kw):
    return pl.pallas_call(
        kernel,
        out_shape=out_shape,
        scratch_shapes=list(scratch),
        compiler_params=pltpu.CompilerParams(vmem_limit_bytes=24 << 20),
        **kw,
    )


def on_device(
    log_rate,
    state,
    excess,
    normal_stress,
    rate_param,
    state_param,
    slip_length,
    self_stiffness,
    damping,
    blocks,
    pattern,
    counts,
):
    patches = log_rate.shape[0]
    flat = (patches // LANES, LANES)
    row_count = lax.axis_size("row")
    col_count = lax.axis_size("col")
    slots, tile_size = blocks.shape[2:]
    shape = jax.ShapeDtypeStruct

    tiles = blocks.reshape(slots, tile_size)
    places = pattern.reshape(slots, 2).T
    more = [
        a.reshape(flat)
        for a in (normal_stress, rate_param, state_param, slip_length, self_stiffness, damping)
    ]
    rate_log = log_rate.reshape(flat)
    state = state.reshape(flat)
    stress = excess.reshape(flat)
    vmem = pl.BlockSpec(memory_space=pltpu.VMEM)
    hbm = pl.BlockSpec(memory_space=pltpu.HBM)

    def far(x):
        return pltpu.with_memory_space_constraint(x, pltpu.HBM)

    def exchange(x, axis):
        return lax.all_to_all(x, axis, split_axis=0, concat_axis=0, tiled=True)

    pushed, index = call(
        push_kernel,
        (shape((col_count,) + flat, bf16), shape((8, slots), jnp.int32)),
        (pltpu.VMEM(flat, f32), pltpu.VMEM((2, slots), jnp.int32), pltpu.SemaphoreType.DMA((2,))),
        in_specs=[hbm, hbm, pl.BlockSpec(memory_space=pltpu.SMEM)],
    )(far(rate_log), far(places), counts)
    parts = pltpu.VMEM((slots, LANES), bf16)
    for step_index in range(STEPS):
        row_rates = exchange(pushed, "col")
        near = [pltpu.VMEM((slots, tile_size), bf16), pltpu.SemaphoreType.DMA((slots // ROWS,))]
        mixed = call(
            mirror_kernel,
            shape((row_count, 2 * flat[0], LANES), bf16),
            [pltpu.VMEM((LANES, tile_size), bf16), parts] + ([] if step_index else near),
            in_specs=[vmem if step_index else hbm, vmem, vmem, vmem],
        )(tiles if step_index else far(tiles), index, row_rates, pushed)
        got = exchange(mixed, "row")
        direct = call(
            direct_kernel,
            shape((col_count,) + flat, bf16),
            (pltpu.VMEM((tile_size, LANES), bf16), parts),
        )(tiles, index, got)
        direct = exchange(direct, "col")
        outs = [shape(flat, f32)] * 3
        if step_index < STEPS - 1:
            outs.append(shape((col_count,) + flat, bf16))
        result = call(later_kernel if step_index else first_kernel, tuple(outs))(
            direct, got, rate_log, state, stress, *more
        )
        rate_log, state, stress = result[:3]
        pushed = result[-1]
    return tuple(a.reshape(patches) for a in (rate_log, state, stress))


def solution(mesh):
    in_specs = (P(("row", "col")),) * 9 + (
        P("row", "col", None, None),
        P("row", "col", None, None),
        P("row", "col"),
    )
    out_specs = (P(("row", "col")), P(("row", "col")), P(("row", "col")))
    return jax.shard_map(
        on_device, mesh=mesh, in_specs=in_specs, out_specs=out_specs, check_vma=False
    )
```

time: 98.3 us -> 94.3 us (0.959)
  blocking collectives: 67.6 us -> 78.8 us
  local copies, waits for them, and re-layouts: 7.09 us -> 0.05 us
  starting transfers between devices: 6.9 us -> 0 us
  waiting for transfers between devices: 1.1 us -> 0 us
    all_to_all x5 -> x6, blocking collectives: 67.6 us -> 78.8 us  [exchange(): return lax.all_to_all(x, axis, split_axis=0, concat_axis=0, tiled=True)]
    unnamed x40 -> x20, local copies, waits for them, and re-layouts: 7.09 us -> 0.05 us
    all_to_all x1 -> x0, starting transfers between devices: 6.9 us -> none  [exchange(): return lax.all_to_all(x, axis, split_axis=0, concat_axis=0, tiled=True)]
    all_to_all x1 -> x0, waiting for transfers between devices: 1.1 us -> none  [exchange(): return lax.all_to_all(x, axis, split_axis=0, concat_axis=0, tiled=True)]
    pallas_call x6 -> x5, Pallas kernels: 12.6 us -> 12.5 us  [the longest x2 6.23 us: on_device(): call(mirror_kernel, shape((row_count, 2 * flat[0], LANES), bf16), [pltpu....]
  transfers between devices with their start and end apart: 1 -> 0, of which waited for: 1 -> 0; matrix products, arithmetic and copies ran while one was open for 0% -> 0% of each run, Pallas kernels for 1% -> 0%
where the time goes in v3:
time: 94.3 us; the launch traced here: 93.9 us
  blocking collectives  78.8 us (84%)
  Pallas kernels  13.5 us (14%)
  between operations  1.57 us (2%)
    all_to_all x6, blocking collectives, exchange(): return lax.all_to_all(x, axis, split_axis=0, concat_axis=0, tiled=True)  78.8 us
    pallas_call x2, Pallas kernels, on_device(): call(mirror_kernel, shape((row_count, 2 * flat[0], LANES), bf16), [pltpu....  6.23 us
    pallas_call x2, Pallas kernels, on_device(): call(direct_kernel, shape((col_count,) + flat, bf16), (pltpu.VMEM((tile_s...  5.31 us

profile of v3, /device:TPU:1, one launch (start us, length us, event | category | flops | bytes accessed | tf_op | source)
XLA Modules:
  0.0 93.9 jit_solution(16643471628819303957)
XLA Ops:
  0.6 0.0 copy-start
  1.4 0.9 shard_map.139
  2.4 12.8 %all_to_all.30.rates = bf16[16,32,128]{2,1,0:T(8,128)(2,1)S(1)} all-to-all(bf16[16,32,128]{2,1,0:T(8,128)(2,1)S(1)} %get-tuple-element.13.pushed), channel_id=1, replica_groups=mesh['row'=16,'col'=16] {'col'}, dimensions={0} | all-to-all | bytes 262144 | tf_op jit(solution)/shard_map/all_to_all | solution.py:227
  15.2 0.0 copy-start.1
  15.2 0.0 copy-start.2
  15.2 0.0 copy-start.3
  15.2 0.0 copy-start.4
  15.2 0.0 copy-start.5
  15.2 0.0 copy-start.6
  15.2 0.0 copy-start.7
  15.2 0.0 copy-start.8
  15.2 0.0 copy-start.9
  15.3 3.7 %shard_map.140 = bf16[16,64,128]{2,1,0:T(8,128)(2,1)S(1)} custom-call(bf16[512,4096]{1,0:T(8,128)(2,1)} %bitcast.16, s32[8,512]{1,0:T(8,128)S(1)} %get-tuple-element.12.index, bf16[16,32,128]{2,1,0:T(8,128)(2,1)S(1)} %all_to_all.30.rates, bf16[16,32,128]{2,1,0:T(8,128)(2,1)S(1)} %get-tuple-element.13.pushed), custom_call_target="tpu_custom_call" | custom-call | tf_op jit(solution)/shard_map/pallas_call | solution.py:239
  19.0 20.5 %all_to_all.31.got = bf16[16,64,128]{2,1,0:T(8,128)(2,1)S(1)} all-to-all(bf16[16,64,128]{2,1,0:T(8,128)(2,1)S(1)} %shard_map.140), channel_id=1, replica_groups=mesh['row'=16,'col'=16] {'row'}, dimensions={0} | all-to-all | bytes 524288 | tf_op jit(solution)/shard_map/all_to_all | solution.py:227
  39.5 0.0 copy-done
  39.5 2.7 %shard_map.141 = bf16[16,32,128]{2,1,0:T(8,128)(2,1)S(1)} custom-call(bf16[512,4096]{1,0:T(8,128)(2,1)S(1)} %bitcast.17, s32[8,512]{1,0:T(8,128)S(1)} %get-tuple-element.12.index, bf16[16,64,128]{2,1,0:T(8,128)(2,1)S(1)} %all_to_all.31.got), custom_call_target="tpu_custom_call" | custom-call | tf_op jit(solution)/shard_map/pallas_call | solution.py:246
  42.2 10.9 %all_to_all.32.direct = bf16[16,32,128]{2,1,0:T(8,128)(2,1)S(1)} all-to-all(bf16[16,32,128]{2,1,0:T(8,128)(2,1)S(1)} %shard_map.141), channel_id=1, replica_groups=mesh['row'=16,'col'=16] {'col'}, dimensions={0} | all-to-all | bytes 262144 | tf_op jit(solution)/shard_map/all_to_all | solution.py:227
  53.1 0.0 copy-done.1
  53.1 0.0 copy-done.2
  53.1 0.0 copy-done.3
  53.1 0.0 copy-done.4
  53.1 0.0 copy-done.5
  53.1 0.0 copy-done.6
  53.1 0.0 copy-done.7
  53.1 0.0 copy-done.8
  53.2 0.0 copy-done.9
  53.2 0.2 shard_map.142
  53.4 9.3 %all_to_all.33.rates = bf16[16,32,128]{2,1,0:T(8,128)(2,1)S(1)} all-to-all(bf16[16,32,128]{2,1,0:T(8,128)(2,1)S(1)} %get-tuple-element.14.pushed), channel_id=1, replica_groups=mesh['row'=16,'col'=16] {'col'}, dimensions={0} | all-to-all | bytes 262144 | tf_op jit(solution)/shard_map/all_to_all | solution.py:227
  62.7 2.5 %shard_map.143 = bf16[16,64,128]{2,1,0:T(8,128)(2,1)S(1)} custom-call(bf16[512,4096]{1,0:T(8,128)(2,1)S(1)} %bitcast.18, s32[8,512]{1,0:T(8,128)S(1)} %get-tuple-element.12.index, bf16[16,32,128]{2,1,0:T(8,128)(2,1)S(1)} %all_to_all.33.rates, bf16[16,32,128]{2,1,0:T(8,128)(2,1)S(1)} %get-tuple-element.14.pushed), custom_call_target="tpu_custom_call" | custom-call | tf_op jit(solution)/shard_map/pallas_call | solution.py:239
  65.2 14.3 %all_to_all.34.got = bf16[16,64,128]{2,1,0:T(8,128)(2,1)S(1)} all-to-all(bf16[16,64,128]{2,1,0:T(8,128)(2,1)S(1)} %shard_map.143), channel_id=1, replica_groups=mesh['row'=16,'col'=16] {'row'}, dimensions={0} | all-to-all | bytes 524288 | tf_op jit(solution)/shard_map/all_to_all | solution.py:227
  79.5 2.7 %shard_map.144 = bf16[16,32,128]{2,1,0:T(8,128)(2,1)S(1)} custom-call(bf16[512,4096]{1,0:T(8,128)(2,1)S(1)} %bitcast.19, s32[8,512]{1,0:T(8,128)S(1)} %get-tuple-element.12.index, bf16[16,64,128]{2,1,0:T(8,128)(2,1)S(1)} %all_to_all.34.got), custom_call_target="tpu_custom_call" | custom-call | tf_op jit(solution)/shard_map/pallas_call | solution.py:246
  82.2 10.9 %all_to_all.35.direct = bf16[16,32,128]{2,1,0:T(8,128)(2,1)S(1)} all-to-all(bf16[16,32,128]{2,1,0:T(8,128)(2,1)S(1)} %shard_map.144), channel_id=1, replica_groups=mesh['row'=16,'col'=16] {'col'}, dimensions={0} | all-to-all | bytes 262144 | tf_op jit(solution)/shard_map/all_to_all | solution.py:227
  93.1 0.8 shard_map.145
Async XLA Ops:
  0.6 38.9 %copy-start = (bf16[1,1,512,4096]{3,2,1,0:T(8,128)(2,1)S(1)}, bf16[1,1,512,4096]{3,2,1,0:T(8,128)(2,1)}, u32[]{:S(2)}) copy-start(bf16[1,1,512,4096]{3,2,1,0:T(8,128)(2,1)} %param.21) | copy-start | bytes 12582916
  15.2 37.9 %copy-start.1 = (f32[4096]{0:T(1024)S(1)}, f32[4096]{0:T(1024)}, u32[]{:S(2)}) copy-start(f32[4096]{0:T(1024)} %param.15) | copy-start | bytes 49156
  15.2 37.9 %copy-start.2 = (f32[4096]{0:T(1024)S(1)}, f32[4096]{0:T(1024)}, u32[]{:S(2)}) copy-start(f32[4096]{0:T(1024)} %param.16) | copy-start | bytes 49156
  15.2 37.9 %copy-start.3 = (f32[4096]{0:T(1024)S(1)}, f32[4096]{0:T(1024)}, u32[]{:S(2)}) copy-start(f32[4096]{0:T(1024)} %param.17) | copy-start | bytes 49156
  15.2 37.9 %copy-start.4 = (f32[4096]{0:T(1024)S(1)}, f32[4096]{0:T(1024)}, u32[]{:S(2)}) copy-start(f32[4096]{0:T(1024)} %param.18) | copy-start | bytes 49156
  15.2 37.9 %copy-start.5 = (f32[4096]{0:T(1024)S(1)}, f32[4096]{0:T(1024)}, u32[]{:S(2)}) copy-start(f32[4096]{0:T(1024)} %param.19) | copy-start | bytes 49156
  15.2 37.9 %copy-start.6 = (f32[4096]{0:T(1024)S(1)}, f32[4096]{0:T(1024)}, u32[]{:S(2)}) copy-start(f32[4096]{0:T(1024)} %param.20) | copy-start | bytes 49156
  15.2 37.9 %copy-start.7 = (f32[4096]{0:T(1024)S(1)}, f32[4096]{0:T(1024)}, u32[]{:S(2)}) copy-start(f32[4096]{0:T(1024)} %param.12) | copy-start | bytes 49156
  15.2 37.9 %copy-start.8 = (f32[4096]{0:T(1024)S(1)}, f32[4096]{0:T(1024)}, u32[]{:S(2)}) copy-start(f32[4096]{0:T(1024)} %param.13) | copy-start | bytes 49156
  15.2 37.9 %copy-start.9 = (f32[4096]{0:T(1024)S(1)}, f32[4096]{0:T(1024)}, u32[]{:S(2)}) copy-start(f32[4096]{0:T(1024)} %param.14) | copy-start | bytes 49156

commit v4 on v3

v4 whole, which is shorter than its diff:
```python
import functools

import jax
import jax.numpy as jnp
from jax import lax
from jax.experimental import pallas as pl
from jax.experimental.pallas import tpu as pltpu
from jax.sharding import PartitionSpec as P

STEPS = 2
NEWTON = 4
TILE = 64
LANES = 128
WIDTH = 256
SPAN = 512

time_step = 0.25
bf16 = jnp.bfloat16
f32 = jnp.float32


def friction_solve(rate_log, stress, state, normal_stress, rate_param, damping):
    strength = normal_stress * rate_param
    lift = state / rate_param
    for turn_index in range(NEWTON):
        speed = jnp.exp(rate_log)
        ratio = 0.5 * jnp.exp(rate_log + lift)
        root = jnp.sqrt(1.0 + ratio * ratio)
        misfit = stress - damping * speed - strength * jnp.log(ratio + root)
        slope = -damping * speed - strength * ratio / root
        rate_log = rate_log - misfit / slope
    return rate_log


def push_kernel(log_rate, pushed_out):
    pushed = (jnp.exp(log_rate[...]) - 1.0).astype(bf16)
    pushed_out[...] = jnp.broadcast_to(pushed[None], pushed_out.shape)


def turn_kernel(segment, tiles_far, places_far, counts, turned, index_out, tiles, sems, places, place_sem):
    place_copy = pltpu.make_async_copy(places_far, places, place_sem)
    place_copy.start()
    copies = fetch(tiles_far, tiles, sems, 0)
    place_copy.wait()
    row_slot, col_slot = places[0:1, :], places[1:2, :]
    live = lax.broadcasted_iota(jnp.int32, row_slot.shape, 1) < counts[0, 0]
    own = col_slot // segment == lax.axis_index("row")
    own = own & (row_slot == lax.axis_index("col") * segment + col_slot % segment)
    index_out[0:1, :] = jnp.where(live, row_slot, -2)
    index_out[1:2, :] = jnp.where(live, col_slot, -2)
    index_out[2:3, :] = jnp.where(live & jnp.logical_not(own), col_slot, -2)
    for turn, copy in enumerate(copies):
        copy.wait()
        lanes = slice(turn * SPAN, turn * SPAN + SPAN)
        turned[lanes, :] = jnp.transpose(tiles[:, lanes])


def fetch(tiles_far, tiles, sems, begin):
    copies = []
    for turn, start in enumerate(range(0, tiles.shape[1], SPAN)):
        copies.append(
            pltpu.make_async_copy(
                tiles_far.at[:, pl.ds(begin + start, SPAN)],
                tiles.at[:, pl.ds(start, SPAN)],
                sems.at[turn],
            )
        )
        copies[-1].start()
    return copies


def one_hot(index, rows):
    tall = lax.broadcasted_iota(jnp.int32, (rows, index.shape[1]), 0)
    return jnp.where(tall == (index >> 1), 1.0, 0.0).astype(bf16)


def chosen(index, rates):
    rates = rates.reshape(-1, LANES)
    both = lax.dot_general(
        rates,
        one_hot(index, rates.shape[0]),
        (((0,), (0,)), ((), ())),
        preferred_element_type=f32,
    )
    return jnp.where((index & 1) == 0, both[:TILE, :], both[TILE:, :])


def dropped(index, sums, rows):
    even = (index & 1) == 0
    halves = jnp.concatenate([jnp.where(even, sums, 0.0), jnp.where(even, 0.0, sums)], axis=0)
    return dot_nt(one_hot(index, rows), halves.astype(bf16)).astype(bf16)


def dot_nt(left, right):
    return lax.dot_general(left, right, (((1,), (1,)), ((), ())), preferred_element_type=f32)


def mirror_sums(columns, index, rates, total):
    rate = total.at[1]
    rate[...] = chosen(index, rates)
    fold = lax.broadcasted_iota(jnp.int32, (TILE, WIDTH), 1) % TILE
    fold = jnp.where(fold == lax.broadcasted_iota(jnp.int32, (TILE, WIDTH), 0), 1.0, 0.0).astype(bf16)
    sums = jnp.zeros((TILE, index.shape[1]), f32)
    for first in range(0, TILE, WIDTH // TILE):
        product = []
        for i in range(first, first + WIDTH // TILE):
            wide = jnp.broadcast_to(rate[i : i + 1, :], sums.shape).astype(bf16)
            product.append(columns(i) * wide)
        sums += jnp.dot(fold, jnp.concatenate(product, axis=0), preferred_element_type=f32)
    return sums


def finish_mirror(sums, index, pushed, out):
    patches = pushed.shape[1]
    total = dropped(index[2:3, :], sums, pushed.shape[0] * patches)
    out[:, :patches, :] = total.reshape(pushed.shape)
    out[:, patches:, :] = pushed[...]


def first_mirror_kernel(tiles_far, early, index, rates, pushed, out, late, tiles, total, sems):
    begin = early.shape[0]
    copies = fetch(tiles_far, tiles, sems, begin)
    held = []

    def columns(i):
        start = i * TILE
        if start < begin:
            return early[start : start + TILE, :]
        start -= begin
        if start % SPAN == 0:
            copies[start // SPAN].wait()
            held[:] = [jnp.transpose(tiles[:, start : start + SPAN])]
            late[start : start + SPAN, :] = held[0]
        return held[0][start % SPAN : start % SPAN + TILE, :]

    finish_mirror(mirror_sums(columns, index[0:1, :], rates[...], total), index, pushed, out)


def later_mirror_kernel(early, late, index, rates, pushed, out, total):
    def columns(i):
        start = i * TILE
        if start < early.shape[0]:
            return early[start : start + TILE, :]
        start -= early.shape[0]
        return late[start : start + TILE, :]

    finish_mirror(mirror_sums(columns, index[0:1, :], rates[...], total), index, pushed, out)


def direct_kernel(early, late, index, got, out):
    patches = out.shape[1]
    rate = chosen(index[1:2, :], got[:, patches:, :]).astype(bf16)
    add = lax.broadcasted_iota(jnp.int32, (8, SPAN), 1) // TILE
    add = jnp.where(add == lax.broadcasted_iota(jnp.int32, (8, SPAN), 0), 1.0, 0.0).astype(bf16)
    rate = jnp.concatenate([rate] * (SPAN // TILE), axis=0)
    sums = [
        jnp.dot(add, turned[start : start + SPAN, :] * rate, preferred_element_type=f32)
        for turned in (early, late)
        for start in range(0, turned.shape[0], SPAN)
    ]
    sums = jnp.concatenate(sums, axis=0)
    out[...] = dropped(index[0:1, :], sums, out.shape[0] * patches).reshape(out.shape)


def step_body(stress, direct, got, rate_log, state, more, outs):
    normal_stress, rate_param, state_param, slip_length, self_stiffness, damping = (m[...] for m in more)
    rate_out, state_out, stress_out, *pushed_out = outs
    stress_rate = jnp.sum(direct[...].astype(f32), axis=0) + jnp.sum(
        got[:, : direct.shape[1], :].astype(f32), axis=0
    )
    speed = jnp.exp(rate_log)
    new_stress = stress + time_step * (stress_rate - self_stiffness * (speed - 1.0))
    new_state = state + time_step * (state_param / slip_length) * (jnp.exp(-state / state_param) - speed)
    new_rate = friction_solve(rate_log, new_stress, new_state, normal_stress, rate_param, damping)
    rate_out[...] = new_rate
    state_out[...] = new_state
    stress_out[...] = new_stress
    for out in pushed_out:
        pushed = (jnp.exp(new_rate) - 1.0).astype(bf16)
        out[...] = jnp.broadcast_to(pushed[None], out.shape)


def first_kernel(direct, got, log_rate, state, excess, *refs):
    more, outs = refs[:6], refs[6:]
    normal_stress, rate_param, damping = more[0][...], more[1][...], more[5][...]
    rate_log, begin = log_rate[...], state[...]
    ratio = 0.5 * jnp.exp(rate_log + begin / rate_param)
    balance = normal_stress * rate_param * jnp.log(ratio + jnp.sqrt(1.0 + ratio * ratio)) + damping * jnp.exp(
        rate_log
    )
    step_body(balance * (1.0 + excess[...]), direct, got, rate_log, begin, more, outs)


def later_kernel(direct, got, rate_log, state, stress, *refs):
    step_body(stress[...], direct, got, rate_log[...], state[...], refs[:6], refs[6:])


def call(kernel, out_shape, scratch=(), **kw):
    return pl.pallas_call(
        kernel,
        out_shape=out_shape,
        scratch_shapes=list(scratch),
        compiler_params=pltpu.CompilerParams(vmem_limit_bytes=24 << 20),
        **kw,
    )


def on_device(
    log_rate,
    state,
    excess,
    normal_stress,
    rate_param,
    state_param,
    slip_length,
    self_stiffness,
    damping,
    blocks,
    pattern,
    counts,
):
    patches = log_rate.shape[0]
    flat = (patches // LANES, LANES)
    row_count = lax.axis_size("row")
    col_count = lax.axis_size("col")
    slots, tile_size = blocks.shape[2:]
    shape = jax.ShapeDtypeStruct

    tiles = blocks.reshape(slots, tile_size)
    places = pattern.reshape(slots, 2).T
    more = [
        a.reshape(flat)
        for a in (normal_stress, rate_param, state_param, slip_length, self_stiffness, damping)
    ]
    rate_log = log_rate.reshape(flat)
    state = state.reshape(flat)
    stress = excess.reshape(flat)
    vmem = pl.BlockSpec(memory_space=pltpu.VMEM)
    hbm = pl.BlockSpec(memory_space=pltpu.HBM)

    def far(x):
        return pltpu.with_memory_space_constraint(x, pltpu.HBM)

    def exchange(x, axis):
        return lax.all_to_all(x, axis, split_axis=0, concat_axis=0, tiled=True)

    pushed = call(push_kernel, shape((col_count,) + flat, bf16), )(far(rate_log))
    half = tile_size // 2
    landing = (
        pltpu.VMEM((slots, half), bf16),
        pltpu.SemaphoreType.DMA((half // SPAN,)),
    )
    turned = (shape((half, slots), bf16),)
    early, index = call(
        functools.partial(turn_kernel, patches // TILE),
        turned + (shape((8, slots), jnp.int32),),
        landing + (pltpu.VMEM((2, slots), jnp.int32), pltpu.SemaphoreType.DMA),
        in_specs=[hbm, hbm, pl.BlockSpec(memory_space=pltpu.SMEM)],
    )(far(tiles), far(places), counts)
    total = pltpu.VMEM((2, TILE, slots), f32)
    mixed_shape = shape((row_count, 2 * flat[0], LANES), bf16)
    for step_index in range(STEPS):
        row_rates = exchange(pushed, "col")
        if step_index:
            mixed = call(later_mirror_kernel, mixed_shape, (total,))(early, late, index, row_rates, pushed)
        else:
            mixed, late = call(
                first_mirror_kernel,
                (mixed_shape,) + turned,
                (landing[0], total, landing[1]),
                in_specs=[hbm, vmem, vmem, vmem, vmem],
            )(far(tiles), early, index, row_rates, pushed)
        got = exchange(mixed, "row")
        direct = call(direct_kernel, shape((col_count,) + flat, bf16))(early, late, index, got)
        direct = exchange(direct, "col")
        outs = [shape(flat, f32)] * 3
        if step_index < STEPS - 1:
            outs.append(shape((col_count,) + flat, bf16))
        result = call(later_kernel if step_index else first_kernel, tuple(outs))(
            direct, got, rate_log, state, stress, *more
        )
        rate_log, state, stress = result[:3]
        pushed = result[-1]
    return tuple(a.reshape(patches) for a in (rate_log, state, stress))


def solution(mesh):
    in_specs = (P(("row", "col")),) * 9 + (
        P("row", "col", None, None),
        P("row", "col", None, None),
        P("row", "col"),
    )
    out_specs = (P(("row", "col")), P(("row", "col")), P(("row", "col")))
    return jax.shard_map(
        on_device, mesh=mesh, in_specs=in_specs, out_specs=out_specs, check_vma=False
    )
```

time: 94.3 us -> 89.7 us (0.951)
  blocking collectives: 78.8 us -> 66 us
  starting transfers between devices: 0 us -> 6.9 us
  waiting for transfers between devices: 0 us -> 3.41 us
  Pallas kernels: 13.5 us -> 11.5 us
    all_to_all x6 -> x5, blocking collectives: 78.8 us -> 66 us  [exchange(): return lax.all_to_all(x, axis, split_axis=0, concat_axis=0, tiled=True)]
    all_to_all x0 -> x1, starting transfers between devices: none -> 6.9 us  [exchange(): return lax.all_to_all(x, axis, split_axis=0, concat_axis=0, tiled=True)]
    all_to_all x0 -> x1, waiting for transfers between devices: none -> 3.41 us  [exchange(): return lax.all_to_all(x, axis, split_axis=0, concat_axis=0, tiled=True)]
    pallas_call x5 -> x6, Pallas kernels: 12.5 us -> 10.5 us  [the longest x1 3.28 us: on_device(): call(first_mirror_kernel, (mixed_shape,) + turned, (landing[0], total, la...]
  transfers between devices with their start and end apart: 0 -> 1, of which waited for: 0 -> 1; matrix products, arithmetic and copies ran while one was open for 0% -> 0% of each run, Pallas kernels for 0% -> 2%
where the time goes in v4:
time: 89.7 us; the launch traced here: 89.2 us
  blocking collectives  66 us (74%)
  Pallas kernels  11.5 us (13%)
  starting transfers between devices  6.9 us (8%)
  waiting for transfers between devices  3.41 us (4%)
  between operations  1.42 us (2%)
    all_to_all x5, blocking collectives, exchange(): return lax.all_to_all(x, axis, split_axis=0, concat_axis=0, tiled=True)  66 us
    all_to_all x1, starting transfers between devices, exchange(): return lax.all_to_all(x, axis, split_axis=0, concat_axis=0, tiled=True)  6.9 us
    all_to_all x1, waiting for transfers between devices, exchange(): return lax.all_to_all(x, axis, split_axis=0, concat_axis=0, tiled=True)  3.41 us
    pallas_call x1, Pallas kernels, on_device(): call(first_mirror_kernel, (mixed_shape,) + turned, (landing[0], total, la...  3.28 us
    pallas_call x2, Pallas kernels, on_device(): call(direct_kernel, shape((col_count,) + flat, bf16))  2.39 us
    pallas_call x1, Pallas kernels, on_device(): call(functools.partial(turn_kernel, patches // TILE), turned + (shape((8,...  2.04 us
  transfers between devices with their start and end apart: 1, of which 1 were waited for; matrix products, arithmetic and copies ran while one was open for 0% of the time, Pallas kernels for 2%

profile of v4, /device:TPU:1, one launch (start us, length us, event | category | flops | bytes accessed | tf_op | source)
XLA Modules:
  0.0 89.2 jit_solution(11234228505963605249)
XLA Ops:
  0.6 1.4 %shard_map.140.pushed = bf16[16,32,128]{2,1,0:T(8,128)(2,1)} custom-call(f32[32,128]{1,0:T(8,128)} %bitcast.16), custom_call_target="tpu_custom_call" | custom-call | tf_op jit(solution)/shard_map/pallas_call | solution.py:247
  2.0 6.9 %all-to-all-start = ((bf16[16,32,128]{2,1,0:T(8,128)(2,1)}), bf16[16,32,128]{2,1,0:T(8,128)(2,1)S(1)}, u32[]{:S(2)}, u32[]{:S(2)}) async-start(bf16[16,32,128]{2,1,0:T(8,128)(2,1)} %shard_map.140.pushed), calls=%async_computation | async-start | bytes 262144 | tf_op jit(solution)/shard_map/all_to_all | solution.py:245
  9.6 2.0 %shard_map.139 = (bf16[2048,512]{1,0:T(8,128)(2,1)S(1)}, s32[8,512]{1,0:T(8,128)S(1)}) custom-call(bf16[512,4096]{1,0:T(8,128)(2,1)} %bitcast.32, s32[2,512]{1,0:T(2,128)} %bitcast.34, s32[1,1]{1,0:T(1,128)S(6)} %copy.15.counts), custom_call_target="tpu_custom_call" | custom-call | tf_op jit(solution)/shard_map/pallas_call | solution.py:254
  11.6 3.4 %all-to-all-done.rates = bf16[16,32,128]{2,1,0:T(8,128)(2,1)S(1)} async-done(((bf16[16,32,128]{2,1,0:T(8,128)(2,1)}), bf16[16,32,128]{2,1,0:T(8,128)(2,1)S(1)}, u32[]{:S(2)}, u32[]{:S(2)}) %all-to-all-start) | async-done | bytes 131104 | tf_op jit(solution)/shard_map/all_to_all | solution.py:245
  15.0 3.3 %shard_map.141 = (bf16[16,64,128]{2,1,0:T(8,128)(2,1)S(1)}, bf16[2048,512]{1,0:T(8,128)(2,1)S(1)}) custom-call(bf16[512,4096]{1,0:T(8,128)(2,1)} %bitcast.33, bf16[2048,512]{1,0:T(8,128)(2,1)S(1)} %get-tuple-element.14.early, s32[8,512]{1,0:T(8,128)S(1)} %get-tuple-element.15.index, bf16[16,32,128]{2,1,0:T(8,128)(2,1)S(1)} %all-to-all-done.rates, ...), custom_call_target="tpu_custom_call" | custom-call | tf_op jit(solution)/shard_map/pallas_call | solution.py:267
  18.3 20.5 %all_to_all.30.got = bf16[16,64,128]{2,1,0:T(8,128)(2,1)S(1)} all-to-all(bf16[16,64,128]{2,1,0:T(8,128)(2,1)S(1)} %get-tuple-element.17), channel_id=1, replica_groups=mesh['row'=16,'col'=16] {'row'}, dimensions={0} | all-to-all | bytes 524288 | tf_op jit(solution)/shard_map/all_to_all | solution.py:245
  38.9 0.0 copy-start
  38.9 0.0 copy-start.1
  38.9 0.0 copy-start.2
  38.9 0.0 copy-start.3
  38.9 0.0 copy-start.4
  38.9 0.0 copy-start.5
  38.9 0.0 copy-start.6
  38.9 0.0 copy-start.7
  38.9 0.0 copy-start.8
  38.9 1.2 %shard_map.142 = bf16[16,32,128]{2,1,0:T(8,128)(2,1)S(1)} custom-call(bf16[2048,512]{1,0:T(8,128)(2,1)S(1)} %get-tuple-element.14.early, bf16[2048,512]{1,0:T(8,128)(2,1)S(1)} %get-tuple-element.16.late, s32[8,512]{1,0:T(8,128)S(1)} %get-tuple-element.15.index, bf16[16,64,128]{2,1,0:T(8,128)(2,1)S(1)} %all_to_all.30.got), custom_call_target="tpu_custom_call" | custom-call | tf_op jit(solution)/shard_map/pallas_call | solution.py:274
  40.1 10.9 %all_to_all.31.direct = bf16[16,32,128]{2,1,0:T(8,128)(2,1)S(1)} all-to-all(bf16[16,32,128]{2,1,0:T(8,128)(2,1)S(1)} %shard_map.142), channel_id=1, replica_groups=mesh['row'=16,'col'=16] {'col'}, dimensions={0} | all-to-all | bytes 262144 | tf_op jit(solution)/shard_map/all_to_all | solution.py:245
  51.1 0.0 copy-done
  51.1 0.0 copy-done.1
  51.1 0.0 copy-done.2
  51.1 0.0 copy-done.3
  51.1 0.0 copy-done.4
  51.1 0.0 copy-done.5
  51.1 0.0 copy-done.6
  51.1 0.0 copy-done.7
  51.1 0.0 copy-done.8
  51.1 0.2 shard_map.143
  51.4 9.3 %all_to_all.32.rates = bf16[16,32,128]{2,1,0:T(8,128)(2,1)S(1)} all-to-all(bf16[16,32,128]{2,1,0:T(8,128)(2,1)S(1)} %get-tuple-element.18.pushed), channel_id=1, replica_groups=mesh['row'=16,'col'=16] {'col'}, dimensions={0} | all-to-all | bytes 262144 | tf_op jit(solution)/shard_map/all_to_all | solution.py:245
  60.6 1.4 %shard_map.144 = bf16[16,64,128]{2,1,0:T(8,128)(2,1)S(1)} custom-call(bf16[2048,512]{1,0:T(8,128)(2,1)S(1)} %get-tuple-element.14.early, bf16[2048,512]{1,0:T(8,128)(2,1)S(1)} %get-tuple-element.16.late, s32[8,512]{1,0:T(8,128)S(1)} %get-tuple-element.15.index, bf16[16,32,128]{2,1,0:T(8,128)(2,1)S(1)} %all_to_all.32.rates, ...), custom_call_target="tpu_custom_call" | custom-call | tf_op jit(solution)/shard_map/pallas_call | solution.py:265
  62.0 14.3 %all_to_all.33.got = bf16[16,64,128]{2,1,0:T(8,128)(2,1)S(1)} all-to-all(bf16[16,64,128]{2,1,0:T(8,128)(2,1)S(1)} %shard_map.144), channel_id=1, replica_groups=mesh['row'=16,'col'=16] {'row'}, dimensions={0} | all-to-all | bytes 524288 | tf_op jit(solution)/shard_map/all_to_all | solution.py:245
  76.3 1.2 %shard_map.145 = bf16[16,32,128]{2,1,0:T(8,128)(2,1)S(1)} custom-call(bf16[2048,512]{1,0:T(8,128)(2,1)S(1)} %get-tuple-element.14.early, bf16[2048,512]{1,0:T(8,128)(2,1)S(1)} %get-tuple-element.16.late, s32[8,512]{1,0:T(8,128)S(1)} %get-tuple-element.15.index, bf16[16,64,128]{2,1,0:T(8,128)(2,1)S(1)} %all_to_all.33.got), custom_call_target="tpu_custom_call" | custom-call | tf_op jit(solution)/shard_map/pallas_call | solution.py:274
  77.5 10.9 %all_to_all.34.direct = bf16[16,32,128]{2,1,0:T(8,128)(2,1)S(1)} all-to-all(bf16[16,32,128]{2,1,0:T(8,128)(2,1)S(1)} %shard_map.145), channel_id=1, replica_groups=mesh['row'=16,'col'=16] {'col'}, dimensions={0} | all-to-all | bytes 262144 | tf_op jit(solution)/shard_map/all_to_all | solution.py:245
  88.4 0.8 shard_map.146
Async XLA Ops:
  2.0 13.0 %all-to-all-start = ((bf16[16,32,128]{2,1,0:T(8,128)(2,1)}), bf16[16,32,128]{2,1,0:T(8,128)(2,1)S(1)}, u32[]{:S(2)}, u32[]{:S(2)}) async-start(bf16[16,32,128]{2,1,0:T(8,128)(2,1)} %shard_map.140.pushed), calls=%async_computation | async-start | bytes 262144 | tf_op jit(solution)/shard_map/all_to_all | solution.py:245
  38.9 12.2 %copy-start = (f32[4096]{0:T(1024)S(1)}, f32[4096]{0:T(1024)}, u32[]{:S(2)}) copy-start(f32[4096]{0:T(1024)} %param.12) | copy-start | bytes 49156
  38.9 12.2 %copy-start.1 = (f32[4096]{0:T(1024)S(1)}, f32[4096]{0:T(1024)}, u32[]{:S(2)}) copy-start(f32[4096]{0:T(1024)} %param.15) | copy-start | bytes 49156
  38.9 12.2 %copy-start.2 = (f32[4096]{0:T(1024)S(1)}, f32[4096]{0:T(1024)}, u32[]{:S(2)}) copy-start(f32[4096]{0:T(1024)} %param.16) | copy-start | bytes 49156
  38.9 12.2 %copy-start.3 = (f32[4096]{0:T(1024)S(1)}, f32[4096]{0:T(1024)}, u32[]{:S(2)}) copy-start(f32[4096]{0:T(1024)} %param.17) | copy-start | bytes 49156
  38.9 12.2 %copy-start.4 = (f32[4096]{0:T(1024)S(1)}, f32[4096]{0:T(1024)}, u32[]{:S(2)}) copy-start(f32[4096]{0:T(1024)} %param.18) | copy-start | bytes 49156
  38.9 12.2 %copy-start.5 = (f32[4096]{0:T(1024)S(1)}, f32[4096]{0:T(1024)}, u32[]{:S(2)}) copy-start(f32[4096]{0:T(1024)} %param.19) | copy-start | bytes 49156
  38.9 12.2 %copy-start.6 = (f32[4096]{0:T(1024)S(1)}, f32[4096]{0:T(1024)}, u32[]{:S(2)}) copy-start(f32[4096]{0:T(1024)} %param.20) | copy-start | bytes 49156
  38.9 12.2 %copy-start.7 = (f32[4096]{0:T(1024)S(1)}, f32[4096]{0:T(1024)}, u32[]{:S(2)}) copy-start(f32[4096]{0:T(1024)} %param.13) | copy-start | bytes 49156
  38.9 12.2 %copy-start.8 = (f32[4096]{0:T(1024)S(1)}, f32[4096]{0:T(1024)}, u32[]{:S(2)}) copy-start(f32[4096]{0:T(1024)} %param.14) | copy-start | bytes 49156

commit v5 on v4

--- a/solution.py
+++ b/solution.py
@@ -13,6 +13,8 @@
 LANES = 128
 WIDTH = 256
 SPAN = 512
+
+ORDER = {"row": 12, "col": 13}
 
 time_step = 0.25
 bf16 = jnp.bfloat16
@@ -46,6 +48,8 @@
     live = lax.broadcasted_iota(jnp.int32, row_slot.shape, 1) < counts[0, 0]
     own = col_slot // segment == lax.axis_index("row")
     own = own & (row_slot == lax.axis_index("col") * segment + col_slot % segment)
+    row_slot = row_slot ^ (segment * ORDER["col"])
+    col_slot = col_slot ^ (segment * ORDER["row"])
     index_out[0:1, :] = jnp.where(live, row_slot, -2)
     index_out[1:2, :] = jnp.where(live, col_slot, -2)
     index_out[2:3, :] = jnp.where(live & jnp.logical_not(own), col_slot, -2)
@@ -110,14 +114,15 @@
     return sums
 
 
-def finish_mirror(sums, index, pushed, out):
-    patches = pushed.shape[1]
-    total = dropped(index[2:3, :], sums, pushed.shape[0] * patches)
-    out[:, :patches, :] = total.reshape(pushed.shape)
-    out[:, patches:, :] = pushed[...]
-
-
-def first_mirror_kernel(tiles_far, early, index, rates, pushed, out, late, tiles, total, sems):
+def finish_mirror(sums, index, rates, out):
+    groups, patches = rates.shape[:2]
+    total = dropped(index[2:3, :], sums, groups * patches)
+    out[:, :patches, :] = total.reshape(rates.shape)
+    own = rates[pl.ds(lax.axis_index("col") ^ ORDER["col"], 1), :, :]
+    out[:, patches:, :] = jnp.broadcast_to(own, rates.shape)
+
+
+def first_mirror_kernel(tiles_far, early, index, rates, out, late, total, tiles, sems):
     begin = early.shape[0]
     copies = fetch(tiles_far, tiles, sems, begin)
     held = []
@@ -133,10 +138,10 @@
             late[start : start + SPAN, :] = held[0]
         return held[0][start % SPAN : start % SPAN + TILE, :]
 
-    finish_mirror(mirror_sums(columns, index[0:1, :], rates[...], total), index, pushed, out)
-
-
-def later_mirror_kernel(early, late, index, rates, pushed, out, total):
+    finish_mirror(mirror_sums(columns, index[0:1, :], rates[...], total), index, rates, out)
+
+
+def later_mirror_kernel(early, late, index, rates, out, total):
     def columns(i):
         start = i * TILE
         if start < early.shape[0]:
@@ -144,7 +149,7 @@
         start -= early.shape[0]
         return late[start : start + TILE, :]
 
-    finish_mirror(mirror_sums(columns, index[0:1, :], rates[...], total), index, pushed, out)
+    finish_mirror(mirror_sums(columns, index[0:1, :], rates[...], total), index, rates, out)
 
 
 def direct_kernel(early, late, index, got, out):
@@ -242,19 +247,21 @@
         return pltpu.with_memory_space_constraint(x, pltpu.HBM)
 
     def exchange(x, axis):
-        return lax.all_to_all(x, axis, split_axis=0, concat_axis=0, tiled=True)
+        order = [k ^ ORDER[axis] for k in range(x.shape[0])]
+        return lax.all_to_all(
+            x, axis, split_axis=0, concat_axis=0, tiled=True, axis_index_groups=[order]
+        )
 
     pushed = call(push_kernel, shape((col_count,) + flat, bf16), )(far(rate_log))
-    half = tile_size // 2
-    landing = (
-        pltpu.VMEM((slots, half), bf16),
-        pltpu.SemaphoreType.DMA((half // SPAN,)),
-    )
-    turned = (shape((half, slots), bf16),)
+    begin = tile_size // 4 * 3
+
+    def landing(lanes):
+        return (pltpu.VMEM((slots, lanes), bf16), pltpu.SemaphoreType.DMA((lanes // SPAN,)))
+
     early, index = call(
         functools.partial(turn_kernel, patches // TILE),
-        turned + (shape((8, slots), jnp.int32),),
-        landing + (pltpu.VMEM((2, slots), jnp.int32), pltpu.SemaphoreType.DMA),
+        (shape((begin, slots), bf16), shape((8, slots), jnp.int32)),
+        landing(begin) + (pltpu.VMEM((2, slots), jnp.int32), pltpu.SemaphoreType.DMA),
         in_specs=[hbm, hbm, pl.BlockSpec(memory_space=pltpu.SMEM)],
     )(far(tiles), far(places), counts)
     total = pltpu.VMEM((2, TILE, slots), f32)
@@ -262,14 +269,14 @@
     for step_index in range(STEPS):
         row_rates = exchange(pushed, "col")
         if step_index:
-            mixed = call(later_mirror_kernel, mixed_shape, (total,))(early, late, index, row_rates, pushed)
+            mixed = call(later_mirror_kernel, mixed_shape, (total,))(early, late, index, row_rates)
         else:
             mixed, late = call(
                 first_mirror_kernel,
-                (mixed_shape,) + turned,
-                (landing[0], total, landing[1]),
-                in_specs=[hbm, vmem, vmem, vmem, vmem],
-            )(far(tiles), early, index, row_rates, pushed)
+                (mixed_shape, shape((tile_size - begin, slots), bf16)),
+                (total,) + landing(tile_size - begin),
+                in_specs=[hbm, vmem, vmem, vmem],
+            )(far(tiles), early, index, row_rates)
         got = exchange(mixed, "row")
         direct = call(direct_kernel, shape((col_count,) + flat, bf16))(early, late, index, got)
         direct = exchange(direct, "col")

time: 89.7 us -> 82.3 us (0.918)
  blocking collectives: 66 us -> 61.2 us
  waiting for transfers between devices: 3.41 us -> 0.01 us
  starting transfers between devices: 6.9 us -> 8.25 us
    all_to_all x5, blocking collectives: 66 us -> 61.2 us  [exchange(): lax.all_to_all(x, axis, split_axis=0, concat_axis=0, tiled=True, axis_ind...]
    all_to_all x1, waiting for transfers between devices: 3.41 us -> 0.01 us  [exchange(): lax.all_to_all(x, axis, split_axis=0, concat_axis=0, tiled=True, axis_ind...]
    all_to_all x1, starting transfers between devices: 6.9 us -> 8.25 us  [exchange(): lax.all_to_all(x, axis, split_axis=0, concat_axis=0, tiled=True, axis_ind...]
  transfers between devices with their start and end apart: 1 -> 1, of which waited for: 1 -> 0; matrix products, arithmetic and copies ran while one was open for 0% -> 0% of each run, Pallas kernels for 2% -> 3%
where the time goes in v5:
time: 82.3 us; the launch traced here: 81.8 us
  blocking collectives  61.2 us (74%)
  Pallas kernels  10.9 us (13%)
  starting transfers between devices  8.25 us (10%)
  between operations  1.45 us (2%)
    all_to_all x5, blocking collectives, exchange(): lax.all_to_all(x, axis, split_axis=0, concat_axis=0, tiled=True, axis_ind...  61.2 us
    all_to_all x1, starting transfers between devices, exchange(): lax.all_to_all(x, axis, split_axis=0, concat_axis=0, tiled=True, axis_ind...  8.25 us
    pallas_call x1, Pallas kernels, on_device(): call(functools.partial(turn_kernel, patches // TILE), (shape((begin, slot...  2.73 us
    pallas_call x2, Pallas kernels, on_device(): call(direct_kernel, shape((col_count,) + flat, bf16))  2.4 us
    pallas_call x1, Pallas kernels, on_device(): call(first_mirror_kernel, (mixed_shape, shape((tile_size - begin, slots),...  1.93 us
  transfers between devices with their start and end apart: 1, of which 0 were waited for; matrix products, arithmetic and copies ran while one was open for 0% of the time, Pallas kernels for 3%

profile of v5, /device:TPU:1, one launch (start us, length us, event | category | flops | bytes accessed | tf_op | source)
XLA Modules:
  0.0 81.8 jit_solution(16843448753047357739)
XLA Ops:
  0.6 1.4 %shard_map.140 = bf16[16,32,128]{2,1,0:T(8,128)(2,1)} custom-call(f32[32,128]{1,0:T(8,128)} %bitcast.16), custom_call_target="tpu_custom_call" | custom-call | tf_op jit(solution)/shard_map/pallas_call | solution.py:255
  2.0 8.2 %all-to-all-start = ((bf16[16,32,128]{2,1,0:T(8,128)(2,1)}), bf16[16,32,128]{2,1,0:T(8,128)(2,1)S(1)}, u32[]{:S(2)}, u32[]{:S(2)}) async-start(bf16[16,32,128]{2,1,0:T(8,128)(2,1)} %shard_map.140), calls=%async_computation | async-start | bytes 262144 | tf_op jit(solution)/shard_map/all_to_all | solution.py:251
  10.9 2.7 %shard_map.139 = (bf16[3072,512]{1,0:T(8,128)(2,1)S(1)}, s32[8,512]{1,0:T(8,128)S(1)}) custom-call(bf16[512,4096]{1,0:T(8,128)(2,1)} %bitcast.32, s32[2,512]{1,0:T(2,128)} %bitcast.34, s32[1,1]{1,0:T(1,128)S(6)} %copy.15.counts), custom_call_target="tpu_custom_call" | custom-call | tf_op jit(solution)/shard_map/pallas_call | solution.py:261
  13.7 0.0 all-to-all-done.rates
  13.7 1.9 %shard_map.141 = (bf16[16,64,128]{2,1,0:T(8,128)(2,1)S(1)}, bf16[1024,512]{1,0:T(8,128)(2,1)S(1)}) custom-call(bf16[512,4096]{1,0:T(8,128)(2,1)} %bitcast.33, bf16[3072,512]{1,0:T(8,128)(2,1)S(1)} %get-tuple-element.14.early, s32[8,512]{1,0:T(8,128)S(1)} %get-tuple-element.15.index, bf16[16,32,128]{2,1,0:T(8,128)(2,1)S(1)} %all-to-all-done.rates), custom_call_target="tpu_custom_call" | custom-call | tf_op jit(solution)/shard_map/pallas_call | solution.py:274
  15.6 0.0 copy-start
  15.6 0.0 copy-start.1
  15.6 0.0 copy-start.2
  15.6 0.0 copy-start.3
  15.7 0.0 copy-start.4
  15.7 0.0 copy-start.5
  15.7 0.0 copy-start.6
  15.7 0.0 copy-start.7
  15.7 0.0 copy-start.8
  15.7 18.8 %all_to_all.30.got = bf16[16,64,128]{2,1,0:T(8,128)(2,1)S(1)} all-to-all(bf16[16,64,128]{2,1,0:T(8,128)(2,1)S(1)} %get-tuple-element.17), channel_id=1, replica_groups={{192,208,224,240,128,144,160,176,64,80,96,112,0,16,32,48},{193,209,225,..., dimensions={0} | all-to-all | bytes 524288 | tf_op jit(solution)/shard_map/all_to_all | solution.py:251
  34.5 1.2 %shard_map.142 = bf16[16,32,128]{2,1,0:T(8,128)(2,1)S(1)} custom-call(bf16[3072,512]{1,0:T(8,128)(2,1)S(1)} %get-tuple-element.14.early, bf16[1024,512]{1,0:T(8,128)(2,1)S(1)} %get-tuple-element.16.late, s32[8,512]{1,0:T(8,128)S(1)} %get-tuple-element.15.index, bf16[16,64,128]{2,1,0:T(8,128)(2,1)S(1)} %all_to_all.30.got), custom_call_target="tpu_custom_call" | custom-call | tf_op jit(solution)/shard_map/pallas_call | solution.py:281
  35.7 8.8 %all_to_all.31.direct = bf16[16,32,128]{2,1,0:T(8,128)(2,1)S(1)} all-to-all(bf16[16,32,128]{2,1,0:T(8,128)(2,1)S(1)} %shard_map.142), channel_id=1, replica_groups={{13,12,15,14,9,8,11,10,5,4,7,6,1,0,3,2},{29,28,31,30,25,24,27,26,21,20,..., dimensions={0} | all-to-all | bytes 262144 | tf_op jit(solution)/shard_map/all_to_all | solution.py:251
  44.5 0.0 copy-done
  44.5 0.0 copy-done.1
  44.5 0.0 copy-done.2
  44.5 0.0 copy-done.3
  44.5 0.0 copy-done.4
  44.5 0.0 copy-done.5
  44.5 0.0 copy-done.6
  44.6 0.0 copy-done.7
  44.6 0.0 copy-done.8
  44.6 0.2 shard_map.143
  44.8 8.6 %all_to_all.32.rates = bf16[16,32,128]{2,1,0:T(8,128)(2,1)S(1)} all-to-all(bf16[16,32,128]{2,1,0:T(8,128)(2,1)S(1)} %get-tuple-element.18), channel_id=1, replica_groups={{13,12,15,14,9,8,11,10,5,4,7,6,1,0,3,2},{29,28,31,30,25,24,27,26,21,20,..., dimensions={0} | all-to-all | bytes 262144 | tf_op jit(solution)/shard_map/all_to_all | solution.py:251
  53.4 1.4 %shard_map.144 = bf16[16,64,128]{2,1,0:T(8,128)(2,1)S(1)} custom-call(bf16[3072,512]{1,0:T(8,128)(2,1)S(1)} %get-tuple-element.14.early, bf16[1024,512]{1,0:T(8,128)(2,1)S(1)} %get-tuple-element.16.late, s32[8,512]{1,0:T(8,128)S(1)} %get-tuple-element.15.index, bf16[16,32,128]{2,1,0:T(8,128)(2,1)S(1)} %all_to_all.32.rates), custom_call_target="tpu_custom_call" | custom-call | tf_op jit(solution)/shard_map/pallas_call | solution.py:272
  54.8 16.0 %all_to_all.33.got = bf16[16,64,128]{2,1,0:T(8,128)(2,1)S(1)} all-to-all(bf16[16,64,128]{2,1,0:T(8,128)(2,1)S(1)} %shard_map.144), channel_id=1, replica_groups={{192,208,224,240,128,144,160,176,64,80,96,112,0,16,32,48},{193,209,225,..., dimensions={0} | all-to-all | bytes 524288 | tf_op jit(solution)/shard_map/all_to_all | solution.py:251
  70.8 1.2 %shard_map.145 = bf16[16,32,128]{2,1,0:T(8,128)(2,1)S(1)} custom-call(bf16[3072,512]{1,0:T(8,128)(2,1)S(1)} %get-tuple-element.14.early, bf16[1024,512]{1,0:T(8,128)(2,1)S(1)} %get-tuple-element.16.late, s32[8,512]{1,0:T(8,128)S(1)} %get-tuple-element.15.index, bf16[16,64,128]{2,1,0:T(8,128)(2,1)S(1)} %all_to_all.33.got), custom_call_target="tpu_custom_call" | custom-call | tf_op jit(solution)/shard_map/pallas_call | solution.py:281
  72.0 9.0 %all_to_all.34.direct = bf16[16,32,128]{2,1,0:T(8,128)(2,1)S(1)} all-to-all(bf16[16,32,128]{2,1,0:T(8,128)(2,1)S(1)} %shard_map.145), channel_id=1, replica_groups={{13,12,15,14,9,8,11,10,5,4,7,6,1,0,3,2},{29,28,31,30,25,24,27,26,21,20,..., dimensions={0} | all-to-all | bytes 262144 | tf_op jit(solution)/shard_map/all_to_all | solution.py:251
  81.0 0.8 shard_map.146
Async XLA Ops:
  2.0 11.6 %all-to-all-start = ((bf16[16,32,128]{2,1,0:T(8,128)(2,1)}), bf16[16,32,128]{2,1,0:T(8,128)(2,1)S(1)}, u32[]{:S(2)}, u32[]{:S(2)}) async-start(bf16[16,32,128]{2,1,0:T(8,128)(2,1)} %shard_map.140), calls=%async_computation | async-start | bytes 262144 | tf_op jit(solution)/shard_map/all_to_all | solution.py:251
  15.6 28.9 %copy-start = (f32[4096]{0:T(1024)S(1)}, f32[4096]{0:T(1024)}, u32[]{:S(2)}) copy-start(f32[4096]{0:T(1024)} %param.12) | copy-start | bytes 49156
  15.6 28.9 %copy-start.1 = (f32[4096]{0:T(1024)S(1)}, f32[4096]{0:T(1024)}, u32[]{:S(2)}) copy-start(f32[4096]{0:T(1024)} %param.15) | copy-start | bytes 49156
  15.6 28.9 %copy-start.2 = (f32[4096]{0:T(1024)S(1)}, f32[4096]{0:T(1024)}, u32[]{:S(2)}) copy-start(f32[4096]{0:T(1024)} %param.16) | copy-start | bytes 49156
  15.6 28.9 %copy-start.3 = (f32[4096]{0:T(1024)S(1)}, f32[4096]{0:T(1024)}, u32[]{:S(2)}) copy-start(f32[4096]{0:T(1024)} %param.17) | copy-start | bytes 49156
  15.7 28.9 %copy-start.4 = (f32[4096]{0:T(1024)S(1)}, f32[4096]{0:T(1024)}, u32[]{:S(2)}) copy-start(f32[4096]{0:T(1024)} %param.18) | copy-start | bytes 49156
  15.7 28.9 %copy-start.5 = (f32[4096]{0:T(1024)S(1)}, f32[4096]{0:T(1024)}, u32[]{:S(2)}) copy-start(f32[4096]{0:T(1024)} %param.19) | copy-start | bytes 49156
  15.7 28.9 %copy-start.6 = (f32[4096]{0:T(1024)S(1)}, f32[4096]{0:T(1024)}, u32[]{:S(2)}) copy-start(f32[4096]{0:T(1024)} %param.20) | copy-start | bytes 49156
  15.7 28.9 %copy-start.7 = (f32[4096]{0:T(1024)S(1)}, f32[4096]{0:T(1024)}, u32[]{:S(2)}) copy-start(f32[4096]{0:T(1024)} %param.13) | copy-start | bytes 49156
  15.7 28.9 %copy-start.8 = (f32[4096]{0:T(1024)S(1)}, f32[4096]{0:T(1024)}, u32[]{:S(2)}) copy-start(f32[4096]{0:T(1024)} %param.14) | copy-start | bytes 49156

commit v6 on v5

--- a/solution.py
+++ b/solution.py
@@ -42,7 +42,12 @@
 def turn_kernel(segment, tiles_far, places_far, counts, turned, index_out, tiles, sems, places, place_sem):
     place_copy = pltpu.make_async_copy(places_far, places, place_sem)
     place_copy.start()
-    copies = fetch(tiles_far, tiles, sems, 0)
+    copies = []
+    for turn, base in enumerate(range(0, tiles.shape[0], LANES)):
+        rows = pl.ds(base, LANES)
+        far = tiles_far.at[rows, pl.ds(0, tiles.shape[1])]
+        copies.append(pltpu.make_async_copy(far, tiles.at[rows, :], sems.at[turn]))
+        copies[-1].start()
     place_copy.wait()
     row_slot, col_slot = places[0:1, :], places[1:2, :]
     live = lax.broadcasted_iota(jnp.int32, row_slot.shape, 1) < counts[0, 0]
@@ -55,8 +60,10 @@
     index_out[2:3, :] = jnp.where(live & jnp.logical_not(own), col_slot, -2)
     for turn, copy in enumerate(copies):
         copy.wait()
-        lanes = slice(turn * SPAN, turn * SPAN + SPAN)
-        turned[lanes, :] = jnp.transpose(tiles[:, lanes])
+        rows = slice(turn * LANES, turn * LANES + LANES)
+        for start in range(0, tiles.shape[1], SPAN):
+            lanes = slice(start, start + SPAN)
+            turned[lanes, rows] = jnp.transpose(tiles[rows, lanes])
 
 
 def fetch(tiles_far, tiles, sems, begin):
@@ -255,13 +262,13 @@
     pushed = call(push_kernel, shape((col_count,) + flat, bf16), )(far(rate_log))
     begin = tile_size // 4 * 3
 
-    def landing(lanes):
-        return (pltpu.VMEM((slots, lanes), bf16), pltpu.SemaphoreType.DMA((lanes // SPAN,)))
+    def landing(lanes, copies):
+        return (pltpu.VMEM((slots, lanes), bf16), pltpu.SemaphoreType.DMA((copies,)))
 
     early, index = call(
         functools.partial(turn_kernel, patches // TILE),
         (shape((begin, slots), bf16), shape((8, slots), jnp.int32)),
-        landing(begin) + (pltpu.VMEM((2, slots), jnp.int32), pltpu.SemaphoreType.DMA),
+        landing(begin, slots // LANES) + (pltpu.VMEM((2, slots), jnp.int32), pltpu.SemaphoreType.DMA),
         in_specs=[hbm, hbm, pl.BlockSpec(memory_space=pltpu.SMEM)],
     )(far(tiles), far(places), counts)
     total = pltpu.VMEM((2, TILE, slots), f32)
@@ -274,7 +281,7 @@
             mixed, late = call(
                 first_mirror_kernel,
                 (mixed_shape, shape((tile_size - begin, slots), bf16)),
-                (total,) + landing(tile_size - begin),
+                (total,) + landing(tile_size - begin, (tile_size - begin) // SPAN),
                 in_specs=[hbm, vmem, vmem, vmem],
             )(far(tiles), early, index, row_rates)
         got = exchange(mixed, "row")

time: 82.3 us -> 82.3 us (level)
  no operation moved by 1% of the time
where the time goes in v6:
time: 82.3 us; the launch traced here: 81.8 us
  blocking collectives  61.4 us (75%)
  Pallas kernels  10.7 us (13%)
  starting transfers between devices  8.25 us (10%)
  between operations  1.45 us (2%)
    all_to_all x5, blocking collectives, exchange(): lax.all_to_all(x, axis, split_axis=0, concat_axis=0, tiled=True, axis_ind...  61.4 us
    all_to_all x1, starting transfers between devices, exchange(): lax.all_to_all(x, axis, split_axis=0, concat_axis=0, tiled=True, axis_ind...  8.25 us
    pallas_call x1, Pallas kernels, on_device(): call(functools.partial(turn_kernel, patches // TILE), (shape((begin, slot...  2.57 us
    pallas_call x2, Pallas kernels, on_device(): call(direct_kernel, shape((col_count,) + flat, bf16))  2.4 us
    pallas_call x1, Pallas kernels, on_device(): call(first_mirror_kernel, (mixed_shape, shape((tile_size - begin, slots),...  1.93 us
  transfers between devices with their start and end apart: 1, of which 0 were waited for; matrix products, arithmetic and copies ran while one was open for 0% of the time, Pallas kernels for 3%

profile of v6, /device:TPU:1, one launch (start us, length us, event | category | flops | bytes accessed | tf_op | source)
XLA Modules:
  0.0 81.8 jit_solution(14271665201816027754)
XLA Ops:
  0.6 1.4 %shard_map.140 = bf16[16,32,128]{2,1,0:T(8,128)(2,1)} custom-call(f32[32,128]{1,0:T(8,128)} %bitcast.16), custom_call_target="tpu_custom_call" | custom-call | tf_op jit(solution)/shard_map/pallas_call | solution.py:262
  2.0 8.2 %all-to-all-start = ((bf16[16,32,128]{2,1,0:T(8,128)(2,1)}), bf16[16,32,128]{2,1,0:T(8,128)(2,1)S(1)}, u32[]{:S(2)}, u32[]{:S(2)}) async-start(bf16[16,32,128]{2,1,0:T(8,128)(2,1)} %shard_map.140), calls=%async_computation | async-start | bytes 262144 | tf_op jit(solution)/shard_map/all_to_all | solution.py:258
  10.9 2.6 %shard_map.139 = (bf16[3072,512]{1,0:T(8,128)(2,1)S(1)}, s32[8,512]{1,0:T(8,128)S(1)}) custom-call(bf16[512,4096]{1,0:T(8,128)(2,1)} %bitcast.32, s32[2,512]{1,0:T(2,128)} %bitcast.34, s32[1,1]{1,0:T(1,128)S(6)} %copy.15.counts), custom_call_target="tpu_custom_call" | custom-call | tf_op jit(solution)/shard_map/pallas_call | solution.py:268
  13.5 0.0 all-to-all-done.rates
  13.5 1.9 %shard_map.141 = (bf16[16,64,128]{2,1,0:T(8,128)(2,1)S(1)}, bf16[1024,512]{1,0:T(8,128)(2,1)S(1)}) custom-call(bf16[512,4096]{1,0:T(8,128)(2,1)} %bitcast.33, bf16[3072,512]{1,0:T(8,128)(2,1)S(1)} %get-tuple-element.14.early, s32[8,512]{1,0:T(8,128)S(1)} %get-tuple-element.15.index, bf16[16,32,128]{2,1,0:T(8,128)(2,1)S(1)} %all-to-all-done.rates), custom_call_target="tpu_custom_call" | custom-call | tf_op jit(solution)/shard_map/pallas_call | solution.py:281
  15.4 0.0 copy-start
  15.5 0.0 copy-start.1
  15.5 0.0 copy-start.2
  15.5 0.0 copy-start.3
  15.5 0.0 copy-start.4
  15.5 0.0 copy-start.5
  15.5 0.0 copy-start.6
  15.5 0.0 copy-start.7
  15.5 0.0 copy-start.8
  15.5 18.8 %all_to_all.30.got = bf16[16,64,128]{2,1,0:T(8,128)(2,1)S(1)} all-to-all(bf16[16,64,128]{2,1,0:T(8,128)(2,1)S(1)} %get-tuple-element.17), channel_id=1, replica_groups={{192,208,224,240,128,144,160,176,64,80,96,112,0,16,32,48},{193,209,225,..., dimensions={0} | all-to-all | bytes 524288 | tf_op jit(solution)/shard_map/all_to_all | solution.py:258
  34.3 1.2 %shard_map.142 = bf16[16,32,128]{2,1,0:T(8,128)(2,1)S(1)} custom-call(bf16[3072,512]{1,0:T(8,128)(2,1)S(1)} %get-tuple-element.14.early, bf16[1024,512]{1,0:T(8,128)(2,1)S(1)} %get-tuple-element.16.late, s32[8,512]{1,0:T(8,128)S(1)} %get-tuple-element.15.index, bf16[16,64,128]{2,1,0:T(8,128)(2,1)S(1)} %all_to_all.30.got), custom_call_target="tpu_custom_call" | custom-call | tf_op jit(solution)/shard_map/pallas_call | solution.py:288
  35.5 8.8 %all_to_all.31.direct = bf16[16,32,128]{2,1,0:T(8,128)(2,1)S(1)} all-to-all(bf16[16,32,128]{2,1,0:T(8,128)(2,1)S(1)} %shard_map.142), channel_id=1, replica_groups={{13,12,15,14,9,8,11,10,5,4,7,6,1,0,3,2},{29,28,31,30,25,24,27,26,21,20,..., dimensions={0} | all-to-all | bytes 262144 | tf_op jit(solution)/shard_map/all_to_all | solution.py:258
  44.4 0.0 copy-done
  44.4 0.0 copy-done.1
  44.4 0.0 copy-done.2
  44.4 0.0 copy-done.3
  44.4 0.0 copy-done.4
  44.4 0.0 copy-done.5
  44.4 0.0 copy-done.6
  44.4 0.0 copy-done.7
  44.4 0.0 copy-done.8
  44.4 0.2 shard_map.143
  44.7 8.6 %all_to_all.32.rates = bf16[16,32,128]{2,1,0:T(8,128)(2,1)S(1)} all-to-all(bf16[16,32,128]{2,1,0:T(8,128)(2,1)S(1)} %get-tuple-element.18), channel_id=1, replica_groups={{13,12,15,14,9,8,11,10,5,4,7,6,1,0,3,2},{29,28,31,30,25,24,27,26,21,20,..., dimensions={0} | all-to-all | bytes 262144 | tf_op jit(solution)/shard_map/all_to_all | solution.py:258
  53.3 1.4 %shard_map.144 = bf16[16,64,128]{2,1,0:T(8,128)(2,1)S(1)} custom-call(bf16[3072,512]{1,0:T(8,128)(2,1)S(1)} %get-tuple-element.14.early, bf16[1024,512]{1,0:T(8,128)(2,1)S(1)} %get-tuple-element.16.late, s32[8,512]{1,0:T(8,128)S(1)} %get-tuple-element.15.index, bf16[16,32,128]{2,1,0:T(8,128)(2,1)S(1)} %all_to_all.32.rates), custom_call_target="tpu_custom_call" | custom-call | tf_op jit(solution)/shard_map/pallas_call | solution.py:279
  54.6 16.1 %all_to_all.33.got = bf16[16,64,128]{2,1,0:T(8,128)(2,1)S(1)} all-to-all(bf16[16,64,128]{2,1,0:T(8,128)(2,1)S(1)} %shard_map.144), channel_id=1, replica_groups={{192,208,224,240,128,144,160,176,64,80,96,112,0,16,32,48},{193,209,225,..., dimensions={0} | all-to-all | bytes 524288 | tf_op jit(solution)/shard_map/all_to_all | solution.py:258
  70.8 1.2 %shard_map.145 = bf16[16,32,128]{2,1,0:T(8,128)(2,1)S(1)} custom-call(bf16[3072,512]{1,0:T(8,128)(2,1)S(1)} %get-tuple-element.14.early, bf16[1024,512]{1,0:T(8,128)(2,1)S(1)} %get-tuple-element.16.late, s32[8,512]{1,0:T(8,128)S(1)} %get-tuple-element.15.index, bf16[16,64,128]{2,1,0:T(8,128)(2,1)S(1)} %all_to_all.33.got), custom_call_target="tpu_custom_call" | custom-call | tf_op jit(solution)/shard_map/pallas_call | solution.py:288
  72.0 9.0 %all_to_all.34.direct = bf16[16,32,128]{2,1,0:T(8,128)(2,1)S(1)} all-to-all(bf16[16,32,128]{2,1,0:T(8,128)(2,1)S(1)} %shard_map.145), channel_id=1, replica_groups={{13,12,15,14,9,8,11,10,5,4,7,6,1,0,3,2},{29,28,31,30,25,24,27,26,21,20,..., dimensions={0} | all-to-all | bytes 262144 | tf_op jit(solution)/shard_map/all_to_all | solution.py:258
  81.0 0.8 shard_map.146
Async XLA Ops:
  2.0 11.5 %all-to-all-start = ((bf16[16,32,128]{2,1,0:T(8,128)(2,1)}), bf16[16,32,128]{2,1,0:T(8,128)(2,1)S(1)}, u32[]{:S(2)}, u32[]{:S(2)}) async-start(bf16[16,32,128]{2,1,0:T(8,128)(2,1)} %shard_map.140), calls=%async_computation | async-start | bytes 262144 | tf_op jit(solution)/shard_map/all_to_all | solution.py:258
  15.4 28.9 %copy-start = (f32[4096]{0:T(1024)S(1)}, f32[4096]{0:T(1024)}, u32[]{:S(2)}) copy-start(f32[4096]{0:T(1024)} %param.12) | copy-start | bytes 49156
  15.5 28.9 %copy-start.1 = (f32[4096]{0:T(1024)S(1)}, f32[4096]{0:T(1024)}, u32[]{:S(2)}) copy-start(f32[4096]{0:T(1024)} %param.15) | copy-start | bytes 49156
  15.5 28.9 %copy-start.2 = (f32[4096]{0:T(1024)S(1)}, f32[4096]{0:T(1024)}, u32[]{:S(2)}) copy-start(f32[4096]{0:T(1024)} %param.16) | copy-start | bytes 49156
  15.5 28.9 %copy-start.3 = (f32[4096]{0:T(1024)S(1)}, f32[4096]{0:T(1024)}, u32[]{:S(2)}) copy-start(f32[4096]{0:T(1024)} %param.17) | copy-start | bytes 49156
  15.5 28.9 %copy-start.4 = (f32[4096]{0:T(1024)S(1)}, f32[4096]{0:T(1024)}, u32[]{:S(2)}) copy-start(f32[4096]{0:T(1024)} %param.18) | copy-start | bytes 49156
  15.5 28.9 %copy-start.5 = (f32[4096]{0:T(1024)S(1)}, f32[4096]{0:T(1024)}, u32[]{:S(2)}) copy-start(f32[4096]{0:T(1024)} %param.19) | copy-start | bytes 49156
  15.5 28.9 %copy-start.6 = (f32[4096]{0:T(1024)S(1)}, f32[4096]{0:T(1024)}, u32[]{:S(2)}) copy-start(f32[4096]{0:T(1024)} %param.20) | copy-start | bytes 49156
  15.5 28.9 %copy-start.7 = (f32[4096]{0:T(1024)S(1)}, f32[4096]{0:T(1024)}, u32[]{:S(2)}) copy-start(f32[4096]{0:T(1024)} %param.13) | copy-start | bytes 49156
  15.5 28.9 %copy-start.8 = (f32[4096]{0:T(1024)S(1)}, f32[4096]{0:T(1024)}, u32[]{:S(2)}) copy-start(f32[4096]{0:T(1024)} %param.14) | copy-start | bytes 49156

commit v7 on v6

--- a/solution.py
+++ b/solution.py
@@ -260,7 +260,7 @@
         )
 
     pushed = call(push_kernel, shape((col_count,) + flat, bf16), )(far(rate_log))
-    begin = tile_size // 4 * 3
+    begin = tile_size // 8 * 5
 
     def landing(lanes, copies):
         return (pltpu.VMEM((slots, lanes), bf16), pltpu.SemaphoreType.DMA((copies,)))

time: 82.3 us -> 82.5 us (level)
  transfers between devices with their start and end apart: 1 -> 1, of which waited for: 0 -> 1; matrix products, arithmetic and copies ran while one was open for 0% -> 0% of each run, Pallas kernels for 3% -> 3%
where the time goes in v7:
time: 82.5 us; the launch traced here: 82 us
  blocking collectives  61.6 us (75%)
  Pallas kernels  10.6 us (13%)
  starting transfers between devices  8.25 us (10%)
  between operations  1.45 us (2%)
    all_to_all x5, blocking collectives, exchange(): lax.all_to_all(x, axis, split_axis=0, concat_axis=0, tiled=True, axis_ind...  61.6 us
    all_to_all x1, starting transfers between devices, exchange(): lax.all_to_all(x, axis, split_axis=0, concat_axis=0, tiled=True, axis_ind...  8.25 us
    pallas_call x2, Pallas kernels, on_device(): call(direct_kernel, shape((col_count,) + flat, bf16))  2.39 us
    pallas_call x1, Pallas kernels, on_device(): call(functools.partial(turn_kernel, patches // TILE), (shape((begin, slot...  2.26 us
    pallas_call x1, Pallas kernels, on_device(): call(first_mirror_kernel, (mixed_shape, shape((tile_size - begin, slots),...  2.13 us
  transfers between devices with their start and end apart: 1, of which 1 were waited for; matrix products, arithmetic and copies ran while one was open for 0% of the time, Pallas kernels for 3%

profile of v7, /device:TPU:1, one launch (start us, length us, event | category | flops | bytes accessed | tf_op | source)
XLA Modules:
  0.0 82.0 jit_solution(9062721265460353800)
XLA Ops:
  0.6 1.4 %shard_map.140 = bf16[16,32,128]{2,1,0:T(8,128)(2,1)} custom-call(f32[32,128]{1,0:T(8,128)} %bitcast.16), custom_call_target="tpu_custom_call" | custom-call | tf_op jit(solution)/shard_map/pallas_call | solution.py:262
  2.0 8.2 %all-to-all-start = ((bf16[16,32,128]{2,1,0:T(8,128)(2,1)}), bf16[16,32,128]{2,1,0:T(8,128)(2,1)S(1)}, u32[]{:S(2)}, u32[]{:S(2)}) async-start(bf16[16,32,128]{2,1,0:T(8,128)(2,1)} %shard_map.140), calls=%async_computation | async-start | bytes 262144 | tf_op jit(solution)/shard_map/all_to_all | solution.py:258
  10.9 2.3 %shard_map.139 = (bf16[2560,512]{1,0:T(8,128)(2,1)S(1)}, s32[8,512]{1,0:T(8,128)S(1)}) custom-call(bf16[512,4096]{1,0:T(8,128)(2,1)} %bitcast.32, s32[2,512]{1,0:T(2,128)} %bitcast.34, s32[1,1]{1,0:T(1,128)S(6)} %copy.15.counts), custom_call_target="tpu_custom_call" | custom-call | tf_op jit(solution)/shard_map/pallas_call | solution.py:268
  13.2 0.1 all-to-all-done.rates
  13.3 2.1 %shard_map.141 = (bf16[16,64,128]{2,1,0:T(8,128)(2,1)S(1)}, bf16[1536,512]{1,0:T(8,128)(2,1)S(1)}) custom-call(bf16[512,4096]{1,0:T(8,128)(2,1)} %bitcast.33, bf16[2560,512]{1,0:T(8,128)(2,1)S(1)} %get-tuple-element.14.early, s32[8,512]{1,0:T(8,128)S(1)} %get-tuple-element.15.index, bf16[16,32,128]{2,1,0:T(8,128)(2,1)S(1)} %all-to-all-done.rates), custom_call_target="tpu_custom_call" | custom-call | tf_op jit(solution)/shard_map/pallas_call | solution.py:281
  15.4 0.0 copy-start
  15.5 0.0 copy-start.1
  15.5 0.0 copy-start.2
  15.5 0.0 copy-start.3
  15.5 0.0 copy-start.4
  15.5 0.0 copy-start.5
  15.5 0.0 copy-start.6
  15.5 0.0 copy-start.7
  15.5 0.0 copy-start.8
  15.6 18.7 %all_to_all.30.got = bf16[16,64,128]{2,1,0:T(8,128)(2,1)S(1)} all-to-all(bf16[16,64,128]{2,1,0:T(8,128)(2,1)S(1)} %get-tuple-element.17), channel_id=1, replica_groups={{192,208,224,240,128,144,160,176,64,80,96,112,0,16,32,48},{193,209,225,..., dimensions={0} | all-to-all | bytes 524288 | tf_op jit(solution)/shard_map/all_to_all | solution.py:258
  34.3 1.2 %shard_map.142 = bf16[16,32,128]{2,1,0:T(8,128)(2,1)S(1)} custom-call(bf16[2560,512]{1,0:T(8,128)(2,1)S(1)} %get-tuple-element.14.early, bf16[1536,512]{1,0:T(8,128)(2,1)S(1)} %get-tuple-element.16.late, s32[8,512]{1,0:T(8,128)S(1)} %get-tuple-element.15.index, bf16[16,64,128]{2,1,0:T(8,128)(2,1)S(1)} %all_to_all.30.got), custom_call_target="tpu_custom_call" | custom-call | tf_op jit(solution)/shard_map/pallas_call | solution.py:288
  35.5 9.1 %all_to_all.31.direct = bf16[16,32,128]{2,1,0:T(8,128)(2,1)S(1)} all-to-all(bf16[16,32,128]{2,1,0:T(8,128)(2,1)S(1)} %shard_map.142), channel_id=1, replica_groups={{13,12,15,14,9,8,11,10,5,4,7,6,1,0,3,2},{29,28,31,30,25,24,27,26,21,20,..., dimensions={0} | all-to-all | bytes 262144 | tf_op jit(solution)/shard_map/all_to_all | solution.py:258
  44.6 0.0 copy-done
  44.6 0.0 copy-done.1
  44.6 0.0 copy-done.2
  44.6 0.0 copy-done.3
  44.6 0.0 copy-done.4
  44.6 0.0 copy-done.5
  44.6 0.0 copy-done.6
  44.6 0.0 copy-done.7
  44.6 0.0 copy-done.8
  44.6 0.2 shard_map.143
  44.9 8.6 %all_to_all.32.rates = bf16[16,32,128]{2,1,0:T(8,128)(2,1)S(1)} all-to-all(bf16[16,32,128]{2,1,0:T(8,128)(2,1)S(1)} %get-tuple-element.18), channel_id=1, replica_groups={{13,12,15,14,9,8,11,10,5,4,7,6,1,0,3,2},{29,28,31,30,25,24,27,26,21,20,..., dimensions={0} | all-to-all | bytes 262144 | tf_op jit(solution)/shard_map/all_to_all | solution.py:258
  53.5 1.4 %shard_map.144 = bf16[16,64,128]{2,1,0:T(8,128)(2,1)S(1)} custom-call(bf16[2560,512]{1,0:T(8,128)(2,1)S(1)} %get-tuple-element.14.early, bf16[1536,512]{1,0:T(8,128)(2,1)S(1)} %get-tuple-element.16.late, s32[8,512]{1,0:T(8,128)S(1)} %get-tuple-element.15.index, bf16[16,32,128]{2,1,0:T(8,128)(2,1)S(1)} %all_to_all.32.rates), custom_call_target="tpu_custom_call" | custom-call | tf_op jit(solution)/shard_map/pallas_call | solution.py:279
  54.9 16.1 %all_to_all.33.got = bf16[16,64,128]{2,1,0:T(8,128)(2,1)S(1)} all-to-all(bf16[16,64,128]{2,1,0:T(8,128)(2,1)S(1)} %shard_map.144), channel_id=1, replica_groups={{192,208,224,240,128,144,160,176,64,80,96,112,0,16,32,48},{193,209,225,..., dimensions={0} | all-to-all | bytes 524288 | tf_op jit(solution)/shard_map/all_to_all | solution.py:258
  71.0 1.2 %shard_map.145 = bf16[16,32,128]{2,1,0:T(8,128)(2,1)S(1)} custom-call(bf16[2560,512]{1,0:T(8,128)(2,1)S(1)} %get-tuple-element.14.early, bf16[1536,512]{1,0:T(8,128)(2,1)S(1)} %get-tuple-element.16.late, s32[8,512]{1,0:T(8,128)S(1)} %get-tuple-element.15.index, bf16[16,64,128]{2,1,0:T(8,128)(2,1)S(1)} %all_to_all.33.got), custom_call_target="tpu_custom_call" | custom-call | tf_op jit(solution)/shard_map/pallas_call | solution.py:288
  72.2 9.0 %all_to_all.34.direct = bf16[16,32,128]{2,1,0:T(8,128)(2,1)S(1)} all-to-all(bf16[16,32,128]{2,1,0:T(8,128)(2,1)S(1)} %shard_map.145), channel_id=1, replica_groups={{13,12,15,14,9,8,11,10,5,4,7,6,1,0,3,2},{29,28,31,30,25,24,27,26,21,20,..., dimensions={0} | all-to-all | bytes 262144 | tf_op jit(solution)/shard_map/all_to_all | solution.py:258
  81.2 0.8 shard_map.146
Async XLA Ops:
  2.0 11.3 %all-to-all-start = ((bf16[16,32,128]{2,1,0:T(8,128)(2,1)}), bf16[16,32,128]{2,1,0:T(8,128)(2,1)S(1)}, u32[]{:S(2)}, u32[]{:S(2)}) async-start(bf16[16,32,128]{2,1,0:T(8,128)(2,1)} %shard_map.140), calls=%async_computation | async-start | bytes 262144 | tf_op jit(solution)/shard_map/all_to_all | solution.py:258
  15.4 29.1 %copy-start = (f32[4096]{0:T(1024)S(1)}, f32[4096]{0:T(1024)}, u32[]{:S(2)}) copy-start(f32[4096]{0:T(1024)} %param.12) | copy-start | bytes 49156
  15.5 29.1 %copy-start.1 = (f32[4096]{0:T(1024)S(1)}, f32[4096]{0:T(1024)}, u32[]{:S(2)}) copy-start(f32[4096]{0:T(1024)} %param.15) | copy-start | bytes 49156
  15.5 29.1 %copy-start.2 = (f32[4096]{0:T(1024)S(1)}, f32[4096]{0:T(1024)}, u32[]{:S(2)}) copy-start(f32[4096]{0:T(1024)} %param.16) | copy-start | bytes 49156
  15.5 29.1 %copy-start.3 = (f32[4096]{0:T(1024)S(1)}, f32[4096]{0:T(1024)}, u32[]{:S(2)}) copy-start(f32[4096]{0:T(1024)} %param.17) | copy-start | bytes 49156
  15.5 29.1 %copy-start.4 = (f32[4096]{0:T(1024)S(1)}, f32[4096]{0:T(1024)}, u32[]{:S(2)}) copy-start(f32[4096]{0:T(1024)} %param.18) | copy-start | bytes 49156
  15.5 29.1 %copy-start.5 = (f32[4096]{0:T(1024)S(1)}, f32[4096]{0:T(1024)}, u32[]{:S(2)}) copy-start(f32[4096]{0:T(1024)} %param.19) | copy-start | bytes 49156
  15.5 29.1 %copy-start.6 = (f32[4096]{0:T(1024)S(1)}, f32[4096]{0:T(1024)}, u32[]{:S(2)}) copy-start(f32[4096]{0:T(1024)} %param.20) | copy-start | bytes 49156
  15.5 29.1 %copy-start.7 = (f32[4096]{0:T(1024)S(1)}, f32[4096]{0:T(1024)}, u32[]{:S(2)}) copy-start(f32[4096]{0:T(1024)} %param.13) | copy-start | bytes 49156
  15.5 29.1 %copy-start.8 = (f32[4096]{0:T(1024)S(1)}, f32[4096]{0:T(1024)}, u32[]{:S(2)}) copy-start(f32[4096]{0:T(1024)} %param.14) | copy-start | bytes 49156
